TPU v7x, 256 devices: a whole 4x4x8 slice. The times are simulated.
256 devices in a mesh: wide: 32 (over z, y), qa: 4 (over x), qb: 2 (over core).
Axes of the slice: x: 4, y: 4, z: 8, core: 2. Of those that a mesh axis runs over, the one named last changes fastest.
Arguments:
- core_slices: float32 [262144, 256], P(('wide', 'qa', 'qb')), may hold values from -64 to 64
- next_core: float32 [256, 16384], P('wide', ('qa', 'qb')), may hold values from -0.375 to 0.375
Outputs:
- ortho_basis: float32 [262144, 256], P(('wide', 'qa', 'qb'))
- new_core: float32 [256, 16384], P('wide', ('qa', 'qb'))
All inputs are finite; a program needn't handle non-finite values.
Results may differ from a plain program's by a relative error of at most 0.0003.
Values sent between devices are 32-bit elements; how exact they have to be, the bound alone decides.
No kernel may reach another device: no remote copies, remote signals or barrier semaphores. Data moves between devices by JAX's collectives and lax.ppermute only.
A program may use at most 128 MiB of HBM per device.

v0:
```python
import functools

import jax
import jax.numpy as jnp
from jax import lax
from jax.experimental import pallas as pl
from jax.experimental.pallas import tpu as pltpu
from jax.sharding import PartitionSpec as P


HALF = 128
SUB = 8
F32 = jnp.float32
NT = (((1,), (1,)), ((), ()))
NN = (((1,), (0,)), ((), ()))
TN = (((0,), (0,)), ((), ()))


def mul(a, b, dims):
    return lax.dot_general(
        a, b, dims, precision=lax.Precision.HIGHEST, preferred_element_type=F32
    )


def row_of(x, j):
    return jnp.broadcast_to(x[j : j + 1, :], x.shape)


def column_of(x, k):
    return jnp.broadcast_to(x[:, k : k + 1], x.shape)


def eliminate(work_ref, upper_ref, inverse_ref, at):
    groups = HALF // SUB
    lane = lax.broadcasted_iota(jnp.int32, (SUB, HALF), 1)
    place = lax.broadcasted_iota(jnp.int32, (SUB, HALF), 0)
    zero = jnp.zeros((SUB, HALF), F32)
    for b in range(groups):
        first = b * SUB
        inside = (lane >= first) & (lane < first + SUB)
        own = work_ref[first : first + SUB, :]
        columns = [column_of(own, first + j) for j in range(SUB)]
        rows = jnp.where(inside, jnp.where(lane - first == place, 1.0, 0.0), own)
        inverses, across, pivots, pivot_rows = [], [], [], []
        for j in range(SUB):
            pivot = row_of(columns[j], j)
            inverse = 1.0 / pivot
            ratio = jnp.where(place > j, columns[j] * inverse, zero)
            ahead = {}
            for i in range(j + 1, SUB):
                ahead[i] = row_of(columns[i], j)
                columns[i] = columns[i] - ratio * ahead[i]
            pivot_row = row_of(rows, j)
            rows = rows - ratio * pivot_row
            inverses.append(inverse)
            across.append(ahead)
            pivots.append(pivot)
            pivot_rows.append(pivot_row)
        for g in range(b + 1, groups):
            other = work_ref[g * SUB : (g + 1) * SUB, :]
            parts = [column_of(other, first + j) for j in range(SUB)]
            other = jnp.where(inside, zero, other)
            for j in range(SUB):
                ratio = parts[j] * inverses[j]
                for i in range(j + 1, SUB):
                    parts[i] = parts[i] - ratio * across[j][i]
                other = other - ratio * pivot_rows[j]
            work_ref[g * SUB : (g + 1) * SUB, :] = other
        pivot_column = pivots[0]
        for j in range(1, SUB):
            pivot_column = jnp.where(place == j, pivots[j], pivot_column)
        root = jnp.sqrt(pivot_column)
        scale = 1.0 / root
        rows = rows * scale
        upper = jnp.where(lane >= first + SUB, rows, zero)
        for j in range(SUB):
            upper = jnp.where((lane == first + j) & (place <= j), columns[j] * scale, upper)
        upper_ref[at + first : at + first + SUB, at : at + HALF] = upper
        inverse_ref[at + first : at + first + SUB, at : at + HALF] = jnp.where(
            lane < first + SUB, rows, zero
        )


def factor_gram(top, side, end, work_ref, upper_ref, inverse_ref):
    work_ref[...] = top
    eliminate(work_ref, upper_ref, inverse_ref, 0)
    inverse_top = inverse_ref[0:HALF, 0:HALF]
    upper_side = mul(inverse_top, side, NN)
    upper_ref[0:HALF, HALF:] = upper_side
    upper_ref[HALF:, 0:HALF] = jnp.zeros((HALF, HALF), F32)
    work_ref[...] = end - mul(upper_side, upper_side, TN)
    carried = mul(upper_side, inverse_top, TN)
    eliminate(work_ref, upper_ref, inverse_ref, HALF)
    inverse_ref[HALF:, 0:HALF] = -mul(inverse_ref[HALF:, HALF:], carried, NN)
    inverse_ref[0:HALF, HALF:] = jnp.zeros((HALF, HALF), F32)


def two_sum(a, b):
    total = a + b
    other = total - a
    return total, (a - (total - other)) + (b - other)


def part(x, anchor):
    return (x + anchor) - anchor


def bf16_dot(a, b):
    return lax.dot_general(a, b, TN, preferred_element_type=F32)


def corners(shape):
    return (
        lax.broadcasted_iota(jnp.int32, shape, 0),
        lax.broadcasted_iota(jnp.int32, shape, 1),
    )


CHUNK = 256
PIECE = HALF + SUB
ANCHOR = 1.5 * 2.0**17
STEP = 2.0**-7


def pack(mine_ref, theirs_ref, at, square, low):
    row, column = corners((HALF, HALF))
    top, end = square[0:HALF, 0:HALF], square[HALF:, HALF:]
    diagonal = jnp.sum(jnp.where(row == column, end, 0.0), axis=0, keepdims=True)
    side = square[0:HALF, HALF:]
    mixed = jnp.where(row <= column, top, end)
    diagonal = jnp.broadcast_to(diagonal, (SUB, HALF))
    mine_ref[at : at + HALF, :] = jnp.where(low, side, mixed)
    theirs_ref[at : at + HALF, :] = jnp.where(low, mixed, side)
    mine_ref[at + HALF : at + PIECE, :] = diagonal
    theirs_ref[at + HALF : at + PIECE, :] = diagonal


def unpack(mine_ref, theirs_ref, at, low):
    row, column = corners((HALF, HALF))
    mine, theirs = mine_ref[at : at + HALF, :], theirs_ref[at : at + HALF, :]
    side = jnp.where(low, mine, theirs)
    mixed = jnp.where(low, theirs, mine)
    edge = slice(at + HALF, at + HALF + 1)
    diagonal = jnp.where(low, mine_ref[edge, :], theirs_ref[edge, :])
    turned = mixed.T
    top = jnp.where(row <= column, mixed, turned)
    end = jnp.where(row > column, mixed, jnp.where(row < column, turned, diagonal))
    return top, side, end


def gram_kernel(place_ref, core_ref, mine_ref, theirs_ref, exact_ref, cross_ref, rest_ref, missing_ref):
    largest = jnp.max(jnp.abs(core_ref[...].astype(jnp.bfloat16).astype(F32)), axis=0, keepdims=True)
    anchor = jnp.broadcast_to(largest * ANCHOR, (CHUNK, core_ref.shape[1]))
    exact_ref[...] = jnp.zeros_like(exact_ref)
    cross_ref[...] = jnp.zeros_like(cross_ref)
    rest_ref[...] = jnp.zeros_like(rest_ref)
    missing_ref[...] = jnp.zeros_like(missing_ref)

    @pl.loop(0, core_ref.shape[0] // CHUNK)
    def _(step):
        core = core_ref[pl.ds(pl.multiple_of(step * CHUNK, CHUNK), CHUNK), :]
        halved = core.astype(jnp.bfloat16)
        wide = halved.astype(F32)
        missing = core - wide
        missing_high = missing.astype(jnp.bfloat16)
        missing_wide = missing_high.astype(F32)
        low_wide = missing - missing_wide
        missing_low = low_wide.astype(jnp.bfloat16)
        half_low = (0.5 * low_wide).astype(jnp.bfloat16)
        half_missing = (0.5 * missing_wide).astype(jnp.bfloat16)
        a = part(wide, anchor)
        left = wide - a
        b = part(left, anchor * STEP)
        c = left - b
        low = lambda x: x.astype(jnp.bfloat16)
        a16, b16, c16 = low(a), low(b), low(c)
        half_b, half_c = low(0.5 * b), low(0.5 * c)
        exact_ref[...] += bf16_dot(a16, a16)
        cross_ref[...] += bf16_dot(a16, b16)
        rest_ref[...] += bf16_dot(
            jnp.concatenate([a16, b16, b16, half_c], axis=0),
            jnp.concatenate([c16, half_b, c16, c16], axis=0),
        )
        missing_ref[...] += bf16_dot(
            jnp.concatenate([halved, halved, half_missing, missing_high, half_low], axis=0),
            jnp.concatenate([missing_high, missing_low, missing_high, missing_low, missing_low], axis=0),
        )

    cross, rest, missing = cross_ref[...], rest_ref[...], missing_ref[...]
    high, first = two_sum(exact_ref[...], cross)
    high, second = two_sum(high, cross.T)
    high, third = two_sum(high, rest + rest.T)
    low_core = place_ref[1] == 0
    pack(mine_ref, theirs_ref, 0, high, low_core)
    pack(mine_ref, theirs_ref, PIECE, ((first + second) + third) + (missing + missing.T), low_core)


def piece_order(place, rank, own_rows):
    depth = 4
    long = rank // (depth * own_rows)
    source, at = corners((rank, rank))
    quarter, z, row = at // (long * own_rows), at // own_rows % long, at % own_rows
    z = (z & 1) * 4 + (z & 2) + (z >> 2)
    shift = jnp.where(quarter == 1, depth - 1, jnp.where(quarter == 2, 1, jnp.where(quarter == 3, 2, 0)))
    y = (place + shift) & (depth - 1)
    return jnp.where(source == (z * depth + y) * own_rows + row, 1.0, 0.0)


def basis_kernel(scale, place_ref, mine_ref, theirs_ref, core_ref, ortho_ref, factor_ref, work_ref, upper_ref, inverse_ref, lack_ref, other_ref, second_ref):
    low_core = place_ref[1] == 0
    top, side, end = (x * scale for x in unpack(mine_ref, theirs_ref, 0, low_core))
    lack_ref[0:HALF, 0:HALF] = top
    lack_ref[0:HALF, HALF:] = side
    lack_ref[HALF:, 0:HALF] = side.T
    lack_ref[HALF:, HALF:] = end
    factor_gram(top, side, end, work_ref, upper_ref, inverse_ref)

    upper = upper_ref[...]
    anchor = jnp.broadcast_to(jnp.max(jnp.abs(upper), axis=0, keepdims=True) * ANCHOR, upper.shape)
    low = lambda x: x.astype(jnp.bfloat16)
    a = part(upper, anchor)
    left = upper - a
    b = part(left, anchor * STEP)
    left = left - b
    c = part(left, anchor * (STEP * STEP))
    d = left - c
    a16, b16, c16, d16 = low(a), low(b), low(c), low(d)
    half_b, half_c = low(0.5 * b), low(0.5 * c)
    exact = bf16_dot(a16, a16)
    cross = bf16_dot(a16, b16)
    rest = bf16_dot(
        jnp.concatenate([a16, b16, a16, b16, b16, c16, c16], axis=0),
        jnp.concatenate([c16, half_b, d16, c16, d16, half_c, d16], axis=0),
    )
    left, first = two_sum(lack_ref[...], -exact)
    left, second = two_sum(left, -cross)
    left, third = two_sum(left, -cross.T)
    lack_ref[...] = left + (((first + second) + third) - (rest + rest.T))
    top, side, end = (x * scale for x in unpack(mine_ref, theirs_ref, PIECE, low_core))
    lack_ref[0:HALF, 0:HALF] += top
    lack_ref[0:HALF, HALF:] += side
    lack_ref[HALF:, 0:HALF] += side.T
    lack_ref[HALF:, HALF:] += end

    other_ref[...] = mul(mul(inverse_ref[...], lack_ref[...], NN), inverse_ref[...], NT)
    row, column = corners((HALF, HALF))
    unit = jnp.where(row == column, 1.0, 0.0)
    factor_gram(
        unit + other_ref[0:HALF, 0:HALF],
        other_ref[0:HALF, HALF:],
        unit + other_ref[HALF:, HALF:],
        work_ref,
        second_ref,
        lack_ref,
    )
    mine = second_ref[pl.ds(pl.multiple_of(place_ref[0] * SUB, SUB), SUB), :]
    order = piece_order(place_ref[0], core_ref.shape[1], factor_ref.shape[0])
    factor_ref[...] = mul(mul(mine, upper_ref[...], NN), order, NN)
    other_ref[...] = mul(lack_ref[...], inverse_ref[...], NN)

    @pl.loop(0, core_ref.shape[0] // CHUNK)
    def _(step):
        here = pl.ds(pl.multiple_of(step * CHUNK, CHUNK), CHUNK)
        ortho_ref[here, :] = mul(core_ref[here, :], other_ref[...], NT)


def next_kernel(factor_ref, own_ref, right_ref, left_ref, far_low_ref, far_high_ref, out_ref):
    low = lambda x: x.astype(jnp.bfloat16)
    factor = factor_ref[...]
    first = low(factor)
    left = factor - first.astype(F32)
    second = low(left)
    third = low(left - second.astype(F32))
    stacked = jnp.concatenate([first.astype(F32), second.astype(F32), third.astype(F32)], axis=0)
    stacked = low(stacked)
    wide = 256

    for step in range(out_ref.shape[1] // wide):
        here = slice(step * wide, (step + 1) * wide)
        pieces = (own_ref, right_ref, left_ref, far_low_ref, far_high_ref)
        values = jnp.concatenate([piece[:, here] for piece in pieces], axis=0)
        high = low(values)
        rest = low(values - high.astype(F32))
        dot = lambda b: lax.dot_general(stacked, b, NN, preferred_element_type=F32)
        whole = dot(high) + dot(rest)
        out_ref[:, here] = whole[0:SUB] + (whole[SUB : 2 * SUB] + whole[2 * SUB :])


def make_calls(rows, rank, scale, own_rows=SUB):
    tall = jax.ShapeDtypeStruct((rows, rank), F32)
    packed = jax.ShapeDtypeStruct((2 * PIECE, HALF), F32)
    smem = pl.BlockSpec(memory_space=pltpu.SMEM)
    vmem = pl.BlockSpec(memory_space=pltpu.VMEM)
    whole = pltpu.VMEM((rank, rank), F32)
    cost = pl.CostEstimate(
        flops=20 * rows * rank * rank, bytes_accessed=8 * rows * rank, transcendentals=0
    )
    gram = pl.pallas_call(
        gram_kernel,
        out_shape=(packed, packed),
        in_specs=[smem, vmem],
        out_specs=(vmem, vmem),
        scratch_shapes=[whole] * 4,
        cost_estimate=cost,
    )
    basis = pl.pallas_call(
        functools.partial(basis_kernel, scale),
        out_shape=(tall, jax.ShapeDtypeStruct((own_rows, rank), F32)),
        in_specs=[smem] + [vmem] * 3,
        out_specs=(vmem,) * 2,
        scratch_shapes=[pltpu.VMEM((HALF, HALF), F32)] + [whole] * 5,
        cost_estimate=cost,
    )
    return gram, basis


def shifted(value, pairs):
    return lax.ppermute(value, ("wide", "qa", "qb"), pairs)


def add_pairs(x, y):
    high, lost = two_sum(x[:PIECE], y[:PIECE])
    return jnp.concatenate([high, (x[PIECE:] + y[PIECE:]) + lost], axis=0)


def tie(*values):
    return lax.optimization_barrier(values)


def sum_and_spread(place, gram, core_slices, next_core):
    depth = 4
    wide, across, cores = (lax.axis_size(n) for n in ("wide", "qa", "qb"))
    long = wide // depth
    z_bits = lax.axis_index("wide") // depth

    def pairs(source):
        out = []
        for i in range(wide * across * cores):
            z, y, x, core = i // (cores * across * depth), i // (cores * across) % depth, i // cores % across, i % cores
            z2, y2, x2, core2 = source(z, y, x, core)
            out.append(((((z2 % long) * depth + y2 % depth) * across + x2 % across) * cores + core2 % cores, i))
        return out

    def around(value, source):
        one, two, three = (shifted(value, pairs(functools.partial(source, d))) for d in (1, 2, -1))
        return add_pairs(add_pairs(value, two), add_pairs(one, three))

    def partner(value, bit):
        return shifted(value, pairs(lambda z, y, x, core: (z ^ bit, y, x, core)))

    def merge(own, other, bit):
        first = (z_bits & bit) == 0
        return jnp.concatenate([jnp.where(first, own, other), jnp.where(first, other, own)], axis=0)

    def beside(value, d):
        return shifted(value, pairs(lambda z, y, x, core: (z, y + d, x, core)))

    swap = pairs(lambda z, y, x, core: (z, y, x, 1 - core))
    other = partner(next_core, 4)
    mine, theirs = gram(place, core_slices)
    mine = add_pairs(mine, shifted(theirs, swap))
    mine, other = tie(mine, other)
    rows = merge(next_core, other, 4)
    other = partner(rows, 2)
    mine = around(mine, lambda d, z, y, x, core: (z, y, x + d, core) if core == 0 else (z, y + d, x, core))
    mine, other = tie(mine, other)
    rows = merge(rows, other, 2)
    other = partner(rows, 1)
    mine = around(mine, lambda d, z, y, x, core: (z, y, x + d, core) if core == 1 else (z, y + d, x, core))
    mine, other = tie(mine, other)
    rows = merge(rows, other, 1)
    right = beside(rows, -1)
    left = beside(rows, 1)
    other = shifted(mine, pairs(lambda z, y, x, core: (z + 4, y, x, core)))
    mine = add_pairs(mine, other)
    mine = around(mine, lambda d, z, y, x, core: (z + d, y, x, core))
    theirs = shifted(mine, swap)
    mine, theirs, right, left = tie(mine, theirs, right, left)
    half = rows.shape[0] // 2
    far_low, far_high = beside(right[:half], -1), beside(left[half:], 1)
    return (mine, theirs), (rows, right, left, far_low, far_high)


def per_device(core_slices, next_core):
    rows, rank = core_slices.shape
    own_rows = next_core.shape[0]
    total_rows = rows * lax.axis_size("wide") * lax.axis_size("qa") * lax.axis_size("qb")
    gram, basis = make_calls(rows, rank, 1.0 / total_rows, own_rows)
    vmem = pl.BlockSpec(memory_space=pltpu.VMEM)
    place = jnp.stack([lax.axis_index("wide"), lax.axis_index("qb")]).astype(jnp.int32)
    total, pieces = sum_and_spread(place, gram, core_slices, next_core)
    ortho_basis, factor = basis(place, *total, core_slices)
    new_core = pl.pallas_call(
        next_kernel,
        out_shape=jax.ShapeDtypeStruct(next_core.shape, F32),
        in_specs=[vmem] * 6,
        out_specs=vmem,
    )(factor, *pieces)
    return (ortho_basis, new_core)


def solution(mesh):
    return jax.shard_map(
        per_device,
        mesh=mesh,
        in_specs=(P(("wide", "qa", "qb"), None), P("wide", ("qa", "qb"))),
        out_specs=(P(("wide", "qa", "qb"), None), P("wide", ("qa", "qb"))),
        check_vma=False,
    )
```

profile of v0, /device:TPU:32, one launch (start us, length us, event | category | flops | bytes accessed | tf_op | source)
XLA Modules:
  0.0 103.8 jit_solution(11232526509648846377)
XLA Ops:
  1.2 4.9 %shard_map.41 = (f32[272,128]{1,0:T(8,128)}, f32[272,128]{1,0:T(8,128)}) custom-call(s32[2]{0:T(128)} %pad_add_fusion.place_ref, f32[1024,256]{1,0:T(8,128)} %core_ref.3), custom_call_target="tpu_custom_call" | custom-call | flops 1342177280 | bytes 2097152 | tf_op jit(solution)/shard_map/pallas_call | solution.py:360
  6.1 6.4 %collective-permute-start.1 = (f32[8,2048]{1,0:T(8,128)S(1)}, f32[8,2048]{1,0:T(8,128)S(1)}, u32[]{:S(2)}, u32[]{:S(2)}) collective-permute-start(f32[8,2048]{1,0:T(8,128)S(1)} %copy-done.6), channel_id=1, source_target_pairs={{128,0},{129,1},{130,2},{131,3},{132,4},{133,5},{134,6},{135,7},{1... | collective-permute-start | bytes 196616 | tf_op jit(solution)/shard_map/ppermute | solution.py:318
  13.4 2.4 %collective-permute-done.1 = f32[8,2048]{1,0:T(8,128)S(1)} collective-permute-done((f32[8,2048]{1,0:T(8,128)S(1)}, f32[8,2048]{1,0:T(8,128)S(1)}, u32[]{:S(2)}, u32[]{:S(2)}) %collective-permute-start.1) | collective-permute-done | bytes 65568 | tf_op jit(solution)/shard_map/ppermute | solution.py:318
  15.9 1.5 %collective-permute-start.4 = (f32[272,128]{1,0:T(8,128)S(1)}, f32[272,128]{1,0:T(8,128)S(1)}, u32[]{:S(2)}, u32[]{:S(2)}) collective-permute-start(f32[272,128]{1,0:T(8,128)S(1)} %pad_maximum_fusion.2), channel_id=1, source_target_pairs={{6,0},{25,1},{0,2},{27,3},{2,4},{29,5},{4,6},{31,7},{14,8},{1,9},{... | collective-permute-start | bytes 417800 | tf_op jit(solution)/shard_map/ppermute | solution.py:318
  17.4 1.7 %collective-permute-start.3 = (f32[272,128]{1,0:T(8,128)S(1)}, f32[272,128]{1,0:T(8,128)S(1)}, u32[]{:S(2)}, u32[]{:S(2)}) collective-permute-start(f32[272,128]{1,0:T(8,128)S(1)} %pad_maximum_fusion.2), channel_id=1, source_target_pairs={{2,0},{9,1},{4,2},{11,3},{6,4},{13,5},{0,6},{15,7},{10,8},{17,9},{... | collective-permute-start | bytes 417800 | tf_op jit(solution)/shard_map/ppermute | solution.py:318
  19.1 1.8 %collective-permute-start.2 = (f32[272,128]{1,0:T(8,128)S(1)}, f32[272,128]{1,0:T(8,128)S(1)}, u32[]{:S(2)}, u32[]{:S(2)}) collective-permute-start(f32[272,128]{1,0:T(8,128)S(1)} %pad_maximum_fusion.2), channel_id=1, source_target_pairs={{4,0},{17,1},{6,2},{19,3},{0,4},{21,5},{2,6},{23,7},{12,8},{25,9},... | collective-permute-start | bytes 417800 | tf_op jit(solution)/shard_map/ppermute | solution.py:318
  20.9 2.0 %collective-permute-start.5 = (f32[16,2048]{1,0:T(8,128)S(1)}, f32[16,2048]{1,0:T(8,128)S(1)}, u32[]{:S(2)}, u32[]{:S(2)}) collective-permute-start(f32[16,2048]{1,0:T(8,128)S(1)} %pad_maximum_fusion.7), channel_id=1, source_target_pairs={{64,0},{65,1},{66,2},{67,3},{68,4},{69,5},{70,6},{71,7},{72,8},{73... | collective-permute-start | bytes 393224 | tf_op jit(solution)/shard_map/ppermute | solution.py:318
  23.0 2.7 %collective-permute-done.2 = f32[272,128]{1,0:T(8,128)S(1)} collective-permute-done((f32[272,128]{1,0:T(8,128)S(1)}, f32[272,128]{1,0:T(8,128)S(1)}, u32[]{:S(2)}, u32[]{:S(2)}) %collective-permute-start.2) | collective-permute-done | bytes 139296 | tf_op jit(solution)/shard_map/ppermute | solution.py:318
  25.8 1.9 %collective-permute-done.5 = f32[16,2048]{1,0:T(8,128)S(1)} collective-permute-done((f32[16,2048]{1,0:T(8,128)S(1)}, f32[16,2048]{1,0:T(8,128)S(1)}, u32[]{:S(2)}, u32[]{:S(2)}) %collective-permute-start.5) | collective-permute-done | bytes 131104 | tf_op jit(solution)/shard_map/ppermute | solution.py:318
  28.6 2.3 %collective-permute-start.7 = (f32[272,128]{1,0:T(8,128)S(1)}, f32[272,128]{1,0:T(8,128)S(1)}, u32[]{:S(2)}, u32[]{:S(2)}) collective-permute-start(f32[272,128]{1,0:T(8,128)S(1)} %pad_maximum_fusion.3), channel_id=1, source_target_pairs={{8,0},{3,1},{10,2},{5,3},{12,4},{7,5},{14,6},{1,7},{16,8},{11,9},{... | collective-permute-start | bytes 417800 | tf_op jit(solution)/shard_map/ppermute | solution.py:318
  30.8 1.4 %collective-permute-start.6 = (f32[272,128]{1,0:T(8,128)S(1)}, f32[272,128]{1,0:T(8,128)S(1)}, u32[]{:S(2)}, u32[]{:S(2)}) collective-permute-start(f32[272,128]{1,0:T(8,128)S(1)} %pad_maximum_fusion.3), channel_id=1, source_target_pairs={{16,0},{5,1},{18,2},{7,3},{20,4},{1,5},{22,6},{3,7},{24,8},{13,9},... | collective-permute-start | bytes 417800 | tf_op jit(solution)/shard_map/ppermute | solution.py:318
  32.3 2.1 %collective-permute-start.9 = (f32[32,2048]{1,0:T(8,128)S(1)}, f32[32,2048]{1,0:T(8,128)S(1)}, u32[]{:S(2)}, u32[]{:S(2)}) collective-permute-start(f32[32,2048]{1,0:T(8,128)S(1)} %pad_maximum_fusion.1), channel_id=1, source_target_pairs={{32,0},{33,1},{34,2},{35,3},{36,4},{37,5},{38,6},{39,7},{40,8},{41... | collective-permute-start | bytes 786440 | tf_op jit(solution)/shard_map/ppermute | solution.py:318
  34.3 3.1 %collective-permute-done.6 = f32[272,128]{1,0:T(8,128)S(1)} collective-permute-done((f32[272,128]{1,0:T(8,128)S(1)}, f32[272,128]{1,0:T(8,128)S(1)}, u32[]{:S(2)}, u32[]{:S(2)}) %collective-permute-start.6) | collective-permute-done | bytes 139296 | tf_op jit(solution)/shard_map/ppermute | solution.py:318
  37.5 3.0 %collective-permute-done.9 = f32[32,2048]{1,0:T(8,128)S(1)} collective-permute-done((f32[32,2048]{1,0:T(8,128)S(1)}, f32[32,2048]{1,0:T(8,128)S(1)}, u32[]{:S(2)}, u32[]{:S(2)}) %collective-permute-start.9) | collective-permute-done | bytes 262176 | tf_op jit(solution)/shard_map/ppermute | solution.py:318
  40.5 4.9 %collective-permute-start.10 = (f32[272,128]{1,0:T(8,128)S(1)}, f32[272,128]{1,0:T(8,128)S(1)}, u32[]{:S(2)}, u32[]{:S(2)}) collective-permute-start(f32[272,128]{1,0:T(8,128)S(1)} %pad_maximum_fusion.4), channel_id=1, source_target_pairs={{128,0},{129,1},{130,2},{131,3},{132,4},{133,5},{134,6},{135,7},{1... | collective-permute-start | bytes 417800 | tf_op jit(solution)/shard_map/ppermute | solution.py:318
  45.4 4.2 %collective-permute-done.10 = f32[272,128]{1,0:T(8,128)S(1)} collective-permute-done((f32[272,128]{1,0:T(8,128)S(1)}, f32[272,128]{1,0:T(8,128)S(1)}, u32[]{:S(2)}, u32[]{:S(2)}) %collective-permute-start.10) | collective-permute-done | bytes 139296 | tf_op jit(solution)/shard_map/ppermute | solution.py:318
  49.7 4.0 %collective-permute-start.13 = (f32[272,128]{1,0:T(8,128)S(1)}, f32[272,128]{1,0:T(8,128)S(1)}, u32[]{:S(2)}, u32[]{:S(2)}) collective-permute-start(f32[272,128]{1,0:T(8,128)S(1)} %pad_maximum_fusion.5), channel_id=1, source_target_pairs={{224,0},{225,1},{226,2},{227,3},{228,4},{229,5},{230,6},{231,7},{2... | collective-permute-start | bytes 417800 | tf_op jit(solution)/shard_map/ppermute | solution.py:318
  53.7 4.6 %collective-permute-start.11 = (f32[272,128]{1,0:T(8,128)S(1)}, f32[272,128]{1,0:T(8,128)S(1)}, u32[]{:S(2)}, u32[]{:S(2)}) collective-permute-start(f32[272,128]{1,0:T(8,128)S(1)} %pad_maximum_fusion.5), channel_id=1, source_target_pairs={{64,0},{65,1},{66,2},{67,3},{68,4},{69,5},{70,6},{71,7},{72,8},{73... | collective-permute-start | bytes 417800 | tf_op jit(solution)/shard_map/ppermute | solution.py:318
  59.0 2.7 %collective-permute-start.16 = (f32[64,2048]{1,0:T(8,128)S(1)}, f32[64,2048]{1,0:T(8,128)S(1)}, u32[]{:S(2)}, u32[]{:S(2)}) collective-permute-start(f32[64,2048]{1,0:T(8,128)S(1)} %pad_maximum_fusion.own_ref), channel_id=1, source_target_pairs={{8,0},{9,1},{10,2},{11,3},{12,4},{13,5},{14,6},{15,7},{16,8},{17,9... | collective-permute-start | bytes 1572872 | tf_op jit(solution)/shard_map/ppermute | solution.py:318
  61.7 3.7 %collective-permute-done.11 = f32[272,128]{1,0:T(8,128)S(1)} collective-permute-done((f32[272,128]{1,0:T(8,128)S(1)}, f32[272,128]{1,0:T(8,128)S(1)}, u32[]{:S(2)}, u32[]{:S(2)}) %collective-permute-start.11) | collective-permute-done | bytes 139296 | tf_op jit(solution)/shard_map/ppermute | solution.py:318
  66.9 5.5 %collective-permute-done.15.right_ref = f32[64,2048]{1,0:T(8,128)S(1)} collective-permute-done((f32[64,2048]{1,0:T(8,128)S(1)}, f32[64,2048]{1,0:T(8,128)S(1)}, u32[]{:S(2)}, u32[]{:S(2)}) %collective-permute-start.15) | collective-permute-done | bytes 524320 | tf_op jit(solution)/shard_map/ppermute | solution.py:318
  72.5 3.5 %collective-permute-start.18 = (f32[32,2048]{1,0:T(8,128)S(1)}, f32[32,2048]{1,0:T(8,128)S(1)}, u32[]{:S(2)}, u32[]{:S(2)}) collective-permute-start(f32[32,2048]{1,0:T(8,128)S(1)} %slice.127), channel_id=1, source_target_pairs={{8,0},{9,1},{10,2},{11,3},{12,4},{13,5},{14,6},{15,7},{16,8},{17,9... | collective-permute-start | bytes 786440 | tf_op jit(solution)/shard_map/ppermute | solution.py:318
  76.0 24.3 %shard_map.42 = (f32[1024,256]{1,0:T(8,128)}, f32[8,256]{1,0:T(8,128)}) custom-call(s32[2]{0:T(128)} %pad_add_fusion.place_ref, f32[272,128]{1,0:T(8,128)} %copy-done.5, f32[272,128]{1,0:T(8,128)} %copy-done.7, f32[1024,256]{1,0:T(8,128)} %core_ref.3), custom_call_target="tpu_custom_call" | custom-call | flops 1342177280 | bytes 2097152 | tf_op jit(solution)/shard_map/pallas_call | solution.py:392
  101.1 2.6 %shard_map.43 = f32[8,2048]{1,0:T(8,128)} custom-call(f32[8,256]{1,0:T(8,128)} %get-tuple-element.27.factor_ref, f32[64,2048]{1,0:T(8,128)} %copy-done, f32[64,2048]{1,0:T(8,128)} %copy-done.1, f32[64,2048]{1,0:T(8,128)} %copy-done.2, f32[32,2048]{1,0:T(8,128)} %copy-done.3, f32[32,2048]{1,0:T(8,128)} %copy-done.4), custom_call_target="tpu_custom_call" | custom-call | tf_op jit(solution)/shard_map/pallas_call | solution.py:393
  (52 shorter events, 6.0 us)
Async XLA Ops:
  6.1 6.4 %collective-permute-start = (f32[272,128]{1,0:T(8,128)}, f32[272,128]{1,0:T(8,128)S(1)}, u32[]{:S(2)}, u32[]{:S(2)}) collective-permute-start(f32[272,128]{1,0:T(8,128)} %get-tuple-element.17), channel_id=1, source_target_pairs={{1,0},{0,1},{3,2},{2,3},{5,4},{4,5},{7,6},{6,7},{9,8},{8,9},{11,10... | collective-permute-start | bytes 417800 | tf_op jit(solution)/shard_map/ppermute | solution.py:318
  6.1 9.8 %collective-permute-start.1 = (f32[8,2048]{1,0:T(8,128)S(1)}, f32[8,2048]{1,0:T(8,128)S(1)}, u32[]{:S(2)}, u32[]{:S(2)}) collective-permute-start(f32[8,2048]{1,0:T(8,128)S(1)} %copy-done.6), channel_id=1, source_target_pairs={{128,0},{129,1},{130,2},{131,3},{132,4},{133,5},{134,6},{135,7},{1... | collective-permute-start | bytes 196616 | tf_op jit(solution)/shard_map/ppermute | solution.py:318
  15.9 7.1 %collective-permute-start.4 = (f32[272,128]{1,0:T(8,128)S(1)}, f32[272,128]{1,0:T(8,128)S(1)}, u32[]{:S(2)}, u32[]{:S(2)}) collective-permute-start(f32[272,128]{1,0:T(8,128)S(1)} %pad_maximum_fusion.2), channel_id=1, source_target_pairs={{6,0},{25,1},{0,2},{27,3},{2,4},{29,5},{4,6},{31,7},{14,8},{1,9},{... | collective-permute-start | bytes 417800 | tf_op jit(solution)/shard_map/ppermute | solution.py:318
  17.4 5.6 %collective-permute-start.3 = (f32[272,128]{1,0:T(8,128)S(1)}, f32[272,128]{1,0:T(8,128)S(1)}, u32[]{:S(2)}, u32[]{:S(2)}) collective-permute-start(f32[272,128]{1,0:T(8,128)S(1)} %pad_maximum_fusion.2), channel_id=1, source_target_pairs={{2,0},{9,1},{4,2},{11,3},{6,4},{13,5},{0,6},{15,7},{10,8},{17,9},{... | collective-permute-start | bytes 417800 | tf_op jit(solution)/shard_map/ppermute | solution.py:318
  19.1 6.6 %collective-permute-start.2 = (f32[272,128]{1,0:T(8,128)S(1)}, f32[272,128]{1,0:T(8,128)S(1)}, u32[]{:S(2)}, u32[]{:S(2)}) collective-permute-start(f32[272,128]{1,0:T(8,128)S(1)} %pad_maximum_fusion.2), channel_id=1, source_target_pairs={{4,0},{17,1},{6,2},{19,3},{0,4},{21,5},{2,6},{23,7},{12,8},{25,9},... | collective-permute-start | bytes 417800 | tf_op jit(solution)/shard_map/ppermute | solution.py:318
  20.9 6.7 %collective-permute-start.5 = (f32[16,2048]{1,0:T(8,128)S(1)}, f32[16,2048]{1,0:T(8,128)S(1)}, u32[]{:S(2)}, u32[]{:S(2)}) collective-permute-start(f32[16,2048]{1,0:T(8,128)S(1)} %pad_maximum_fusion.7), channel_id=1, source_target_pairs={{64,0},{65,1},{66,2},{67,3},{68,4},{69,5},{70,6},{71,7},{72,8},{73... | collective-permute-start | bytes 393224 | tf_op jit(solution)/shard_map/ppermute | solution.py:318
  27.6 6.7 %collective-permute-start.8 = (f32[272,128]{1,0:T(8,128)S(1)}, f32[272,128]{1,0:T(8,128)S(1)}, u32[]{:S(2)}, u32[]{:S(2)}) collective-permute-start(f32[272,128]{1,0:T(8,128)S(1)} %pad_maximum_fusion.3), channel_id=1, source_target_pairs={{24,0},{7,1},{26,2},{1,3},{28,4},{3,5},{30,6},{5,7},{0,8},{15,9},{... | collective-permute-start | bytes 417800 | tf_op jit(solution)/shard_map/ppermute | solution.py:318
  28.6 5.8 %collective-permute-start.7 = (f32[272,128]{1,0:T(8,128)S(1)}, f32[272,128]{1,0:T(8,128)S(1)}, u32[]{:S(2)}, u32[]{:S(2)}) collective-permute-start(f32[272,128]{1,0:T(8,128)S(1)} %pad_maximum_fusion.3), channel_id=1, source_target_pairs={{8,0},{3,1},{10,2},{5,3},{12,4},{7,5},{14,6},{1,7},{16,8},{11,9},{... | collective-permute-start | bytes 417800 | tf_op jit(solution)/shard_map/ppermute | solution.py:318
  30.8 6.6 %collective-permute-start.6 = (f32[272,128]{1,0:T(8,128)S(1)}, f32[272,128]{1,0:T(8,128)S(1)}, u32[]{:S(2)}, u32[]{:S(2)}) collective-permute-start(f32[272,128]{1,0:T(8,128)S(1)} %pad_maximum_fusion.3), channel_id=1, source_target_pairs={{16,0},{5,1},{18,2},{7,3},{20,4},{1,5},{22,6},{3,7},{24,8},{13,9},... | collective-permute-start | bytes 417800 | tf_op jit(solution)/shard_map/ppermute | solution.py:318
  32.3 8.2 %collective-permute-start.9 = (f32[32,2048]{1,0:T(8,128)S(1)}, f32[32,2048]{1,0:T(8,128)S(1)}, u32[]{:S(2)}, u32[]{:S(2)}) collective-permute-start(f32[32,2048]{1,0:T(8,128)S(1)} %pad_maximum_fusion.1), channel_id=1, source_target_pairs={{32,0},{33,1},{34,2},{35,3},{36,4},{37,5},{38,6},{39,7},{40,8},{41... | collective-permute-start | bytes 786440 | tf_op jit(solution)/shard_map/ppermute | solution.py:318
  40.5 9.2 %collective-permute-start.10 = (f32[272,128]{1,0:T(8,128)S(1)}, f32[272,128]{1,0:T(8,128)S(1)}, u32[]{:S(2)}, u32[]{:S(2)}) collective-permute-start(f32[272,128]{1,0:T(8,128)S(1)} %pad_maximum_fusion.4), channel_id=1, source_target_pairs={{128,0},{129,1},{130,2},{131,3},{132,4},{133,5},{134,6},{135,7},{1... | collective-permute-start | bytes 417800 | tf_op jit(solution)/shard_map/ppermute | solution.py:318
  49.7 12.0 %collective-permute-start.13 = (f32[272,128]{1,0:T(8,128)S(1)}, f32[272,128]{1,0:T(8,128)S(1)}, u32[]{:S(2)}, u32[]{:S(2)}) collective-permute-start(f32[272,128]{1,0:T(8,128)S(1)} %pad_maximum_fusion.5), channel_id=1, source_target_pairs={{224,0},{225,1},{226,2},{227,3},{228,4},{229,5},{230,6},{231,7},{2... | collective-permute-start | bytes 417800 | tf_op jit(solution)/shard_map/ppermute | solution.py:318
  53.7 8.0 %collective-permute-start.12 = (f32[272,128]{1,0:T(8,128)S(1)}, f32[272,128]{1,0:T(8,128)S(1)}, u32[]{:S(2)}, u32[]{:S(2)}) collective-permute-start(f32[272,128]{1,0:T(8,128)S(1)} %pad_maximum_fusion.5), channel_id=1, source_target_pairs={{32,0},{33,1},{34,2},{35,3},{36,4},{37,5},{38,6},{39,7},{40,8},{41... | collective-permute-start | bytes 417800 | tf_op jit(solution)/shard_map/ppermute | solution.py:318
  53.7 11.6 %collective-permute-start.11 = (f32[272,128]{1,0:T(8,128)S(1)}, f32[272,128]{1,0:T(8,128)S(1)}, u32[]{:S(2)}, u32[]{:S(2)}) collective-permute-start(f32[272,128]{1,0:T(8,128)S(1)} %pad_maximum_fusion.5), channel_id=1, source_target_pairs={{64,0},{65,1},{66,2},{67,3},{68,4},{69,5},{70,6},{71,7},{72,8},{73... | collective-permute-start | bytes 417800 | tf_op jit(solution)/shard_map/ppermute | solution.py:318
  58.3 14.0 %copy-start = (f32[64,2048]{1,0:T(8,128)}, f32[64,2048]{1,0:T(8,128)S(1)}, u32[]{:S(2)}) copy-start(f32[64,2048]{1,0:T(8,128)S(1)} %pad_maximum_fusion.own_ref) | copy-start | bytes 1572868
  58.4 14.0 %collective-permute-start.15 = (f32[64,2048]{1,0:T(8,128)S(1)}, f32[64,2048]{1,0:T(8,128)S(1)}, u32[]{:S(2)}, u32[]{:S(2)}) collective-permute-start(f32[64,2048]{1,0:T(8,128)S(1)} %pad_maximum_fusion.own_ref), channel_id=1, source_target_pairs={{24,0},{25,1},{26,2},{27,3},{28,4},{29,5},{30,6},{31,7},{0,8},{1,9... | collective-permute-start | bytes 1572872 | tf_op jit(solution)/shard_map/ppermute | solution.py:318
  59.0 13.3 %collective-permute-start.16 = (f32[64,2048]{1,0:T(8,128)S(1)}, f32[64,2048]{1,0:T(8,128)S(1)}, u32[]{:S(2)}, u32[]{:S(2)}) collective-permute-start(f32[64,2048]{1,0:T(8,128)S(1)} %pad_maximum_fusion.own_ref), channel_id=1, source_target_pairs={{8,0},{9,1},{10,2},{11,3},{12,4},{13,5},{14,6},{15,7},{16,8},{17,9... | collective-permute-start | bytes 1572872 | tf_op jit(solution)/shard_map/ppermute | solution.py:318
  65.4 7.0 %copy-start.5 = (f32[272,128]{1,0:T(8,128)}, f32[272,128]{1,0:T(8,128)S(1)}, u32[]{:S(2)}) copy-start(f32[272,128]{1,0:T(8,128)S(1)} %pad_maximum_fusion.6.mine_ref) | copy-start | bytes 417796
  65.4 1.4 %collective-permute-start.14 = (f32[272,128]{1,0:T(8,128)S(1)}, f32[272,128]{1,0:T(8,128)S(1)}, u32[]{:S(2)}, u32[]{:S(2)}) collective-permute-start(f32[272,128]{1,0:T(8,128)S(1)} %pad_maximum_fusion.6.mine_ref), channel_id=1, source_target_pairs={{1,0},{0,1},{3,2},{2,3},{5,4},{4,5},{7,6},{6,7},{9,8},{8,9},{11,10... | collective-permute-start | bytes 417800 | tf_op jit(solution)/shard_map/ppermute | solution.py:318
  66.9 5.5 %copy-start.7 = (f32[272,128]{1,0:T(8,128)}, f32[272,128]{1,0:T(8,128)S(1)}, u32[]{:S(2)}) copy-start(f32[272,128]{1,0:T(8,128)S(1)} %collective-permute-done.14.theirs_ref) | copy-start | bytes 417796
  72.4 28.0 %copy-start.1 = (f32[64,2048]{1,0:T(8,128)}, f32[64,2048]{1,0:T(8,128)S(1)}, u32[]{:S(2)}) copy-start(f32[64,2048]{1,0:T(8,128)S(1)} %collective-permute-done.15.right_ref) | copy-start | bytes 1572868
  72.4 28.0 %copy-start.2 = (f32[64,2048]{1,0:T(8,128)}, f32[64,2048]{1,0:T(8,128)S(1)}, u32[]{:S(2)}) copy-start(f32[64,2048]{1,0:T(8,128)S(1)} %collective-permute-done.16.left_ref) | copy-start | bytes 1572868
  72.4 27.9 %collective-permute-start.17 = (f32[32,2048]{1,0:T(8,128)S(1)}, f32[32,2048]{1,0:T(8,128)S(1)}, u32[]{:S(2)}, u32[]{:S(2)}) collective-permute-start(f32[32,2048]{1,0:T(8,128)S(1)} %slice.126), channel_id=1, source_target_pairs={{24,0},{25,1},{26,2},{27,3},{28,4},{29,5},{30,6},{31,7},{0,8},{1,9... | collective-permute-start | bytes 786440 | tf_op jit(solution)/shard_map/ppermute | solution.py:318
  72.5 27.8 %collective-permute-start.18 = (f32[32,2048]{1,0:T(8,128)S(1)}, f32[32,2048]{1,0:T(8,128)S(1)}, u32[]{:S(2)}, u32[]{:S(2)}) collective-permute-start(f32[32,2048]{1,0:T(8,128)S(1)} %slice.127), channel_id=1, source_target_pairs={{8,0},{9,1},{10,2},{11,3},{12,4},{13,5},{14,6},{15,7},{16,8},{17,9... | collective-permute-start | bytes 786440 | tf_op jit(solution)/shard_map/ppermute | solution.py:318
  (3 other events, 6.4 us)
where the time goes:
time: 104 us
  starting transfers between devices  40.6 us (39%)
  Pallas kernels  31.8 us (31%)
  waiting for transfers between devices  27.7 us (27%)
  other arithmetic  1.96 us (2%)
    ppermute x19, starting transfers between devices, shifted(): return lax.ppermute(value, ('wide', 'qa', 'qb'), pairs)  40.6 us
    ppermute x19, waiting for transfers between devices, shifted(): return lax.ppermute(value, ('wide', 'qa', 'qb'), pairs)  27.7 us
    pallas_call x1, Pallas kernels, per_device(): ortho_basis, factor = basis(place, *total, core_slices)  24.3 us
    pallas_call x1, Pallas kernels, sum_and_spread(): mine, theirs = gram(place, core_slices)  4.87 us
    pallas_call x1, Pallas kernels, per_device(): pl.pallas_call(next_kernel, out_shape=jax.ShapeDtypeStruct(next_core.shap...  2.65 us
  transfers between devices with their start and end apart: 19, of which 9 were waited for; matrix products, arithmetic and copies ran while one was open for 1% of the time, Pallas kernels for 23%

commit v1 on v0

--- a/solution.py
+++ b/solution.py
@@ -148,7 +148,7 @@
     return top, side, end
 
 
-def gram_kernel(place_ref, core_ref, mine_ref, theirs_ref, exact_ref, cross_ref, rest_ref, missing_ref):
+def gram_kernel(core_ref, mine_ref, theirs_ref, exact_ref, cross_ref, rest_ref, missing_ref):
     largest = jnp.max(jnp.abs(core_ref[...].astype(jnp.bfloat16).astype(F32)), axis=0, keepdims=True)
     anchor = jnp.broadcast_to(largest * ANCHOR, (CHUNK, core_ref.shape[1]))
     exact_ref[...] = jnp.zeros_like(exact_ref)
@@ -190,7 +190,7 @@
     high, first = two_sum(exact_ref[...], cross)
     high, second = two_sum(high, cross.T)
     high, third = two_sum(high, rest + rest.T)
-    low_core = place_ref[1] == 0
+    low_core = lax.axis_index("qb") == 0
     pack(mine_ref, theirs_ref, 0, high, low_core)
     pack(mine_ref, theirs_ref, PIECE, ((first + second) + third) + (missing + missing.T), low_core)
 
@@ -206,8 +206,8 @@
     return jnp.where(source == (z * depth + y) * own_rows + row, 1.0, 0.0)
 
 
-def basis_kernel(scale, place_ref, mine_ref, theirs_ref, core_ref, ortho_ref, factor_ref, work_ref, upper_ref, inverse_ref, lack_ref, other_ref, second_ref):
-    low_core = place_ref[1] == 0
+def basis_kernel(scale, mine_ref, theirs_ref, core_ref, ortho_ref, factor_ref, work_ref, upper_ref, inverse_ref, lack_ref, other_ref, second_ref):
+    low_core = lax.axis_index("qb") == 0
     top, side, end = (x * scale for x in unpack(mine_ref, theirs_ref, 0, low_core))
     lack_ref[0:HALF, 0:HALF] = top
     lack_ref[0:HALF, HALF:] = side
@@ -253,8 +253,9 @@
         second_ref,
         lack_ref,
     )
-    mine = second_ref[pl.ds(pl.multiple_of(place_ref[0] * SUB, SUB), SUB), :]
-    order = piece_order(place_ref[0], core_ref.shape[1], factor_ref.shape[0])
+    at = lax.axis_index("wide")
+    mine = second_ref[pl.ds(pl.multiple_of(at * SUB, SUB), SUB), :]
+    order = piece_order(at, core_ref.shape[1], factor_ref.shape[0])
     factor_ref[...] = mul(mul(mine, upper_ref[...], NN), order, NN)
     other_ref[...] = mul(lack_ref[...], inverse_ref[...], NN)
 
@@ -264,7 +265,7 @@
         ortho_ref[here, :] = mul(core_ref[here, :], other_ref[...], NT)
 
 
-def next_kernel(factor_ref, own_ref, right_ref, left_ref, far_low_ref, far_high_ref, out_ref):
+def next_kernel(factor_ref, own_ref, right_ref, left_ref, far_ref, out_ref):
     low = lambda x: x.astype(jnp.bfloat16)
     factor = factor_ref[...]
     first = low(factor)
@@ -277,7 +278,7 @@
 
     for step in range(out_ref.shape[1] // wide):
         here = slice(step * wide, (step + 1) * wide)
-        pieces = (own_ref, right_ref, left_ref, far_low_ref, far_high_ref)
+        pieces = (own_ref, right_ref, left_ref, far_ref)
         values = jnp.concatenate([piece[:, here] for piece in pieces], axis=0)
         high = low(values)
         rest = low(values - high.astype(F32))
@@ -289,7 +290,6 @@
 def make_calls(rows, rank, scale, own_rows=SUB):
     tall = jax.ShapeDtypeStruct((rows, rank), F32)
     packed = jax.ShapeDtypeStruct((2 * PIECE, HALF), F32)
-    smem = pl.BlockSpec(memory_space=pltpu.SMEM)
     vmem = pl.BlockSpec(memory_space=pltpu.VMEM)
     whole = pltpu.VMEM((rank, rank), F32)
     cost = pl.CostEstimate(
@@ -298,7 +298,7 @@
     gram = pl.pallas_call(
         gram_kernel,
         out_shape=(packed, packed),
-        in_specs=[smem, vmem],
+        in_specs=[vmem],
         out_specs=(vmem, vmem),
         scratch_shapes=[whole] * 4,
         cost_estimate=cost,
@@ -306,7 +306,7 @@
     basis = pl.pallas_call(
         functools.partial(basis_kernel, scale),
         out_shape=(tall, jax.ShapeDtypeStruct((own_rows, rank), F32)),
-        in_specs=[smem] + [vmem] * 3,
+        in_specs=[vmem] * 3,
         out_specs=(vmem,) * 2,
         scratch_shapes=[pltpu.VMEM((HALF, HALF), F32)] + [whole] * 5,
         cost_estimate=cost,
@@ -327,7 +327,7 @@
     return lax.optimization_barrier(values)
 
 
-def sum_and_spread(place, gram, core_slices, next_core):
+def sum_and_spread(gram, core_slices, next_core):
     depth = 4
     wide, across, cores = (lax.axis_size(n) for n in ("wide", "qa", "qb"))
     long = wide // depth
@@ -357,7 +357,7 @@
 
     swap = pairs(lambda z, y, x, core: (z, y, x, 1 - core))
     other = partner(next_core, 4)
-    mine, theirs = gram(place, core_slices)
+    mine, theirs = gram(core_slices)
     mine = add_pairs(mine, shifted(theirs, swap))
     mine, other = tie(mine, other)
     rows = merge(next_core, other, 4)
@@ -371,14 +371,13 @@
     rows = merge(rows, other, 1)
     right = beside(rows, -1)
     left = beside(rows, 1)
+    far = beside(rows, 2)
     other = shifted(mine, pairs(lambda z, y, x, core: (z + 4, y, x, core)))
     mine = add_pairs(mine, other)
     mine = around(mine, lambda d, z, y, x, core: (z + d, y, x, core))
     theirs = shifted(mine, swap)
     mine, theirs, right, left = tie(mine, theirs, right, left)
-    half = rows.shape[0] // 2
-    far_low, far_high = beside(right[:half], -1), beside(left[half:], 1)
-    return (mine, theirs), (rows, right, left, far_low, far_high)
+    return (mine, theirs), (rows, right, left, far)
 
 
 def per_device(core_slices, next_core):
@@ -387,13 +386,12 @@
     total_rows = rows * lax.axis_size("wide") * lax.axis_size("qa") * lax.axis_size("qb")
     gram, basis = make_calls(rows, rank, 1.0 / total_rows, own_rows)
     vmem = pl.BlockSpec(memory_space=pltpu.VMEM)
-    place = jnp.stack([lax.axis_index("wide"), lax.axis_index("qb")]).astype(jnp.int32)
-    total, pieces = sum_and_spread(place, gram, core_slices, next_core)
-    ortho_basis, factor = basis(place, *total, core_slices)
+    total, pieces = sum_and_spread(gram, core_slices, next_core)
+    ortho_basis, factor = basis(*total, core_slices)
     new_core = pl.pallas_call(
         next_kernel,
         out_shape=jax.ShapeDtypeStruct(next_core.shape, F32),
-        in_specs=[vmem] * 6,
+        in_specs=[vmem] * 5,
         out_specs=vmem,
     )(factor, *pieces)
     return (ortho_basis, new_core)

time: 104 us -> 111 us (1.067)
  waiting for transfers between devices: 27.7 us -> 36.1 us
    ppermute x19 -> x18, waiting for transfers between devices: 27.7 us -> 36.1 us  [shifted(): return lax.ppermute(value, ('wide', 'qa', 'qb'), pairs)]
    ppermute x19 -> x18, starting transfers between devices: 40.6 us -> 39.9 us  [shifted(): return lax.ppermute(value, ('wide', 'qa', 'qb'), pairs)]
  transfers between devices with their start and end apart: 19 -> 18, of which waited for: 9 -> 9; matrix products, arithmetic and copies ran while one was open for 1% -> 1% of each run, Pallas kernels for 23% -> 22%
where the time goes in v1:
time: 111 us
  starting transfers between devices  39.9 us (36%)
  waiting for transfers between devices  36.1 us (33%)
  Pallas kernels  32.1 us (29%)
  other arithmetic  1.36 us (1%)
    ppermute x18, starting transfers between devices, shifted(): return lax.ppermute(value, ('wide', 'qa', 'qb'), pairs)  39.9 us
    ppermute x18, waiting for transfers between devices, shifted(): return lax.ppermute(value, ('wide', 'qa', 'qb'), pairs)  36.1 us
    pallas_call x1, Pallas kernels, per_device(): ortho_basis, factor = basis(*total, core_slices)  24.6 us
    pallas_call x1, Pallas kernels, sum_and_spread(): mine, theirs = gram(core_slices)  4.86 us
    pallas_call x1, Pallas kernels, per_device(): pl.pallas_call(next_kernel, out_shape=jax.ShapeDtypeStruct(next_core.shap...  2.66 us
  transfers between devices with their start and end apart: 18, of which 9 were waited for; matrix products, arithmetic and copies ran while one was open for 1% of the time, Pallas kernels for 22%

profile of v1, /device:TPU:32, one launch (start us, length us, event | category | flops | bytes accessed | tf_op | source)
XLA Modules:
  0.0 111.1 jit_solution(13930684318425310223)
XLA Ops:
  0.6 4.9 %shard_map.41 = (f32[272,128]{1,0:T(8,128)}, f32[272,128]{1,0:T(8,128)}) custom-call(f32[1024,256]{1,0:T(8,128)} %core_ref.3), custom_call_target="tpu_custom_call" | custom-call | flops 1342177280 | bytes 2097152 | tf_op jit(solution)/shard_map/pallas_call | solution.py:360
  5.5 6.3 %collective-permute-start.1 = (f32[8,2048]{1,0:T(8,128)S(1)}, f32[8,2048]{1,0:T(8,128)S(1)}, u32[]{:S(2)}, u32[]{:S(2)}) collective-permute-start(f32[8,2048]{1,0:T(8,128)S(1)} %copy-done.5), channel_id=1, source_target_pairs={{128,0},{129,1},{130,2},{131,3},{132,4},{133,5},{134,6},{135,7},{1... | collective-permute-start | bytes 196616 | tf_op jit(solution)/shard_map/ppermute | solution.py:318
  12.8 2.4 %collective-permute-done.1 = f32[8,2048]{1,0:T(8,128)S(1)} collective-permute-done((f32[8,2048]{1,0:T(8,128)S(1)}, f32[8,2048]{1,0:T(8,128)S(1)}, u32[]{:S(2)}, u32[]{:S(2)}) %collective-permute-start.1) | collective-permute-done | bytes 65568 | tf_op jit(solution)/shard_map/ppermute | solution.py:318
  15.2 1.5 %collective-permute-start.4 = (f32[272,128]{1,0:T(8,128)S(1)}, f32[272,128]{1,0:T(8,128)S(1)}, u32[]{:S(2)}, u32[]{:S(2)}) collective-permute-start(f32[272,128]{1,0:T(8,128)S(1)} %pad_maximum_fusion.2), channel_id=1, source_target_pairs={{6,0},{25,1},{0,2},{27,3},{2,4},{29,5},{4,6},{31,7},{14,8},{1,9},{... | collective-permute-start | bytes 417800 | tf_op jit(solution)/shard_map/ppermute | solution.py:318
  16.7 1.7 %collective-permute-start.3 = (f32[272,128]{1,0:T(8,128)S(1)}, f32[272,128]{1,0:T(8,128)S(1)}, u32[]{:S(2)}, u32[]{:S(2)}) collective-permute-start(f32[272,128]{1,0:T(8,128)S(1)} %pad_maximum_fusion.2), channel_id=1, source_target_pairs={{2,0},{9,1},{4,2},{11,3},{6,4},{13,5},{0,6},{15,7},{10,8},{17,9},{... | collective-permute-start | bytes 417800 | tf_op jit(solution)/shard_map/ppermute | solution.py:318
  18.5 1.8 %collective-permute-start.2 = (f32[272,128]{1,0:T(8,128)S(1)}, f32[272,128]{1,0:T(8,128)S(1)}, u32[]{:S(2)}, u32[]{:S(2)}) collective-permute-start(f32[272,128]{1,0:T(8,128)S(1)} %pad_maximum_fusion.2), channel_id=1, source_target_pairs={{4,0},{17,1},{6,2},{19,3},{0,4},{21,5},{2,6},{23,7},{12,8},{25,9},... | collective-permute-start | bytes 417800 | tf_op jit(solution)/shard_map/ppermute | solution.py:318
  20.3 2.0 %collective-permute-start.5 = (f32[16,2048]{1,0:T(8,128)S(1)}, f32[16,2048]{1,0:T(8,128)S(1)}, u32[]{:S(2)}, u32[]{:S(2)}) collective-permute-start(f32[16,2048]{1,0:T(8,128)S(1)} %pad_maximum_fusion.7), channel_id=1, source_target_pairs={{64,0},{65,1},{66,2},{67,3},{68,4},{69,5},{70,6},{71,7},{72,8},{73... | collective-permute-start | bytes 393224 | tf_op jit(solution)/shard_map/ppermute | solution.py:318
  22.4 2.7 %collective-permute-done.2 = f32[272,128]{1,0:T(8,128)S(1)} collective-permute-done((f32[272,128]{1,0:T(8,128)S(1)}, f32[272,128]{1,0:T(8,128)S(1)}, u32[]{:S(2)}, u32[]{:S(2)}) %collective-permute-start.2) | collective-permute-done | bytes 139296 | tf_op jit(solution)/shard_map/ppermute | solution.py:318
  25.1 1.9 %collective-permute-done.5 = f32[16,2048]{1,0:T(8,128)S(1)} collective-permute-done((f32[16,2048]{1,0:T(8,128)S(1)}, f32[16,2048]{1,0:T(8,128)S(1)}, u32[]{:S(2)}, u32[]{:S(2)}) %collective-permute-start.5) | collective-permute-done | bytes 131104 | tf_op jit(solution)/shard_map/ppermute | solution.py:318
  28.0 2.3 %collective-permute-start.7 = (f32[272,128]{1,0:T(8,128)S(1)}, f32[272,128]{1,0:T(8,128)S(1)}, u32[]{:S(2)}, u32[]{:S(2)}) collective-permute-start(f32[272,128]{1,0:T(8,128)S(1)} %pad_maximum_fusion.3), channel_id=1, source_target_pairs={{8,0},{3,1},{10,2},{5,3},{12,4},{7,5},{14,6},{1,7},{16,8},{11,9},{... | collective-permute-start | bytes 417800 | tf_op jit(solution)/shard_map/ppermute | solution.py:318
  30.2 1.4 %collective-permute-start.6 = (f32[272,128]{1,0:T(8,128)S(1)}, f32[272,128]{1,0:T(8,128)S(1)}, u32[]{:S(2)}, u32[]{:S(2)}) collective-permute-start(f32[272,128]{1,0:T(8,128)S(1)} %pad_maximum_fusion.3), channel_id=1, source_target_pairs={{16,0},{5,1},{18,2},{7,3},{20,4},{1,5},{22,6},{3,7},{24,8},{13,9},... | collective-permute-start | bytes 417800 | tf_op jit(solution)/shard_map/ppermute | solution.py:318
  31.7 2.1 %collective-permute-start.9 = (f32[32,2048]{1,0:T(8,128)S(1)}, f32[32,2048]{1,0:T(8,128)S(1)}, u32[]{:S(2)}, u32[]{:S(2)}) collective-permute-start(f32[32,2048]{1,0:T(8,128)S(1)} %pad_maximum_fusion.1), channel_id=1, source_target_pairs={{32,0},{33,1},{34,2},{35,3},{36,4},{37,5},{38,6},{39,7},{40,8},{41... | collective-permute-start | bytes 786440 | tf_op jit(solution)/shard_map/ppermute | solution.py:318
  33.7 3.1 %collective-permute-done.6 = f32[272,128]{1,0:T(8,128)S(1)} collective-permute-done((f32[272,128]{1,0:T(8,128)S(1)}, f32[272,128]{1,0:T(8,128)S(1)}, u32[]{:S(2)}, u32[]{:S(2)}) %collective-permute-start.6) | collective-permute-done | bytes 139296 | tf_op jit(solution)/shard_map/ppermute | solution.py:318
  36.9 3.0 %collective-permute-done.9 = f32[32,2048]{1,0:T(8,128)S(1)} collective-permute-done((f32[32,2048]{1,0:T(8,128)S(1)}, f32[32,2048]{1,0:T(8,128)S(1)}, u32[]{:S(2)}, u32[]{:S(2)}) %collective-permute-start.9) | collective-permute-done | bytes 262176 | tf_op jit(solution)/shard_map/ppermute | solution.py:318
  39.8 4.9 %collective-permute-start.10 = (f32[272,128]{1,0:T(8,128)S(1)}, f32[272,128]{1,0:T(8,128)S(1)}, u32[]{:S(2)}, u32[]{:S(2)}) collective-permute-start(f32[272,128]{1,0:T(8,128)S(1)} %pad_maximum_fusion.4), channel_id=1, source_target_pairs={{128,0},{129,1},{130,2},{131,3},{132,4},{133,5},{134,6},{135,7},{1... | collective-permute-start | bytes 417800 | tf_op jit(solution)/shard_map/ppermute | solution.py:318
  44.8 4.3 %collective-permute-done.10 = f32[272,128]{1,0:T(8,128)S(1)} collective-permute-done((f32[272,128]{1,0:T(8,128)S(1)}, f32[272,128]{1,0:T(8,128)S(1)}, u32[]{:S(2)}, u32[]{:S(2)}) %collective-permute-start.10) | collective-permute-done | bytes 139296 | tf_op jit(solution)/shard_map/ppermute | solution.py:318
  49.1 4.0 %collective-permute-start.13 = (f32[272,128]{1,0:T(8,128)S(1)}, f32[272,128]{1,0:T(8,128)S(1)}, u32[]{:S(2)}, u32[]{:S(2)}) collective-permute-start(f32[272,128]{1,0:T(8,128)S(1)} %pad_maximum_fusion.5), channel_id=1, source_target_pairs={{224,0},{225,1},{226,2},{227,3},{228,4},{229,5},{230,6},{231,7},{2... | collective-permute-start | bytes 417800 | tf_op jit(solution)/shard_map/ppermute | solution.py:318
  53.1 4.6 %collective-permute-start.11 = (f32[272,128]{1,0:T(8,128)S(1)}, f32[272,128]{1,0:T(8,128)S(1)}, u32[]{:S(2)}, u32[]{:S(2)}) collective-permute-start(f32[272,128]{1,0:T(8,128)S(1)} %pad_maximum_fusion.5), channel_id=1, source_target_pairs={{64,0},{65,1},{66,2},{67,3},{68,4},{69,5},{70,6},{71,7},{72,8},{73... | collective-permute-start | bytes 417800 | tf_op jit(solution)/shard_map/ppermute | solution.py:318
  58.3 2.7 %collective-permute-start.16 = (f32[64,2048]{1,0:T(8,128)S(1)}, f32[64,2048]{1,0:T(8,128)S(1)}, u32[]{:S(2)}, u32[]{:S(2)}) collective-permute-start(f32[64,2048]{1,0:T(8,128)S(1)} %pad_maximum_fusion.own_ref), channel_id=1, source_target_pairs={{8,0},{9,1},{10,2},{11,3},{12,4},{13,5},{14,6},{15,7},{16,8},{17,9... | collective-permute-start | bytes 1572872 | tf_op jit(solution)/shard_map/ppermute | solution.py:318
  61.1 2.9 %collective-permute-start.17 = (f32[64,2048]{1,0:T(8,128)S(1)}, f32[64,2048]{1,0:T(8,128)S(1)}, u32[]{:S(2)}, u32[]{:S(2)}) collective-permute-start(f32[64,2048]{1,0:T(8,128)S(1)} %pad_maximum_fusion.own_ref), channel_id=1, source_target_pairs={{16,0},{17,1},{18,2},{19,3},{20,4},{21,5},{22,6},{23,7},{24,8},{25... | collective-permute-start | bytes 1572872 | tf_op jit(solution)/shard_map/ppermute | solution.py:318
  64.9 1.3 %collective-permute-done.14.theirs_ref = f32[272,128]{1,0:T(8,128)S(1)} collective-permute-done((f32[272,128]{1,0:T(8,128)S(1)}, f32[272,128]{1,0:T(8,128)S(1)}, u32[]{:S(2)}, u32[]{:S(2)}) %collective-permute-start.14) | collective-permute-done | bytes 139296 | tf_op jit(solution)/shard_map/ppermute | solution.py:318
  66.3 16.7 %collective-permute-done.15.right_ref = f32[64,2048]{1,0:T(8,128)S(1)} collective-permute-done((f32[64,2048]{1,0:T(8,128)S(1)}, f32[64,2048]{1,0:T(8,128)S(1)}, u32[]{:S(2)}, u32[]{:S(2)}) %collective-permute-start.15) | collective-permute-done | bytes 524320 | tf_op jit(solution)/shard_map/ppermute | solution.py:318
  83.0 24.6 %shard_map.42 = (f32[1024,256]{1,0:T(8,128)}, f32[8,256]{1,0:T(8,128)}) custom-call(f32[272,128]{1,0:T(8,128)} %copy-done.4, f32[272,128]{1,0:T(8,128)} %copy-done.6, f32[1024,256]{1,0:T(8,128)} %core_ref.3), custom_call_target="tpu_custom_call" | custom-call | flops 1342177280 | bytes 2097152 | tf_op jit(solution)/shard_map/pallas_call | solution.py:390
  108.4 2.7 %shard_map.43 = f32[8,2048]{1,0:T(8,128)} custom-call(f32[8,256]{1,0:T(8,128)} %get-tuple-element.27.factor_ref, f32[64,2048]{1,0:T(8,128)} %copy-done, f32[64,2048]{1,0:T(8,128)} %copy-done.1, f32[64,2048]{1,0:T(8,128)} %copy-done.2, f32[64,2048]{1,0:T(8,128)} %copy-done.3), custom_call_target="tpu_custom_call" | custom-call | tf_op jit(solution)/shard_map/pallas_call | solution.py:391
  (45 shorter events, 4.6 us)
Async XLA Ops:
  0.6 4.9 %copy-start.5 = (f32[8,2048]{1,0:T(8,128)S(1)}, f32[8,2048]{1,0:T(8,128)}, u32[]{:S(2)}) copy-start(f32[8,2048]{1,0:T(8,128)} %param.3) | copy-start | bytes 196612
  5.5 6.4 %collective-permute-start = (f32[272,128]{1,0:T(8,128)}, f32[272,128]{1,0:T(8,128)S(1)}, u32[]{:S(2)}, u32[]{:S(2)}) collective-permute-start(f32[272,128]{1,0:T(8,128)} %get-tuple-element.17), channel_id=1, source_target_pairs={{1,0},{0,1},{3,2},{2,3},{5,4},{4,5},{7,6},{6,7},{9,8},{8,9},{11,10... | collective-permute-start | bytes 417800 | tf_op jit(solution)/shard_map/ppermute | solution.py:318
  5.5 9.7 %collective-permute-start.1 = (f32[8,2048]{1,0:T(8,128)S(1)}, f32[8,2048]{1,0:T(8,128)S(1)}, u32[]{:S(2)}, u32[]{:S(2)}) collective-permute-start(f32[8,2048]{1,0:T(8,128)S(1)} %copy-done.5), channel_id=1, source_target_pairs={{128,0},{129,1},{130,2},{131,3},{132,4},{133,5},{134,6},{135,7},{1... | collective-permute-start | bytes 196616 | tf_op jit(solution)/shard_map/ppermute | solution.py:318
  15.2 7.1 %collective-permute-start.4 = (f32[272,128]{1,0:T(8,128)S(1)}, f32[272,128]{1,0:T(8,128)S(1)}, u32[]{:S(2)}, u32[]{:S(2)}) collective-permute-start(f32[272,128]{1,0:T(8,128)S(1)} %pad_maximum_fusion.2), channel_id=1, source_target_pairs={{6,0},{25,1},{0,2},{27,3},{2,4},{29,5},{4,6},{31,7},{14,8},{1,9},{... | collective-permute-start | bytes 417800 | tf_op jit(solution)/shard_map/ppermute | solution.py:318
  16.7 5.6 %collective-permute-start.3 = (f32[272,128]{1,0:T(8,128)S(1)}, f32[272,128]{1,0:T(8,128)S(1)}, u32[]{:S(2)}, u32[]{:S(2)}) collective-permute-start(f32[272,128]{1,0:T(8,128)S(1)} %pad_maximum_fusion.2), channel_id=1, source_target_pairs={{2,0},{9,1},{4,2},{11,3},{6,4},{13,5},{0,6},{15,7},{10,8},{17,9},{... | collective-permute-start | bytes 417800 | tf_op jit(solution)/shard_map/ppermute | solution.py:318
  18.5 6.6 %collective-permute-start.2 = (f32[272,128]{1,0:T(8,128)S(1)}, f32[272,128]{1,0:T(8,128)S(1)}, u32[]{:S(2)}, u32[]{:S(2)}) collective-permute-start(f32[272,128]{1,0:T(8,128)S(1)} %pad_maximum_fusion.2), channel_id=1, source_target_pairs={{4,0},{17,1},{6,2},{19,3},{0,4},{21,5},{2,6},{23,7},{12,8},{25,9},... | collective-permute-start | bytes 417800 | tf_op jit(solution)/shard_map/ppermute | solution.py:318
  20.3 6.7 %collective-permute-start.5 = (f32[16,2048]{1,0:T(8,128)S(1)}, f32[16,2048]{1,0:T(8,128)S(1)}, u32[]{:S(2)}, u32[]{:S(2)}) collective-permute-start(f32[16,2048]{1,0:T(8,128)S(1)} %pad_maximum_fusion.7), channel_id=1, source_target_pairs={{64,0},{65,1},{66,2},{67,3},{68,4},{69,5},{70,6},{71,7},{72,8},{73... | collective-permute-start | bytes 393224 | tf_op jit(solution)/shard_map/ppermute | solution.py:318
  27.0 6.7 %collective-permute-start.8 = (f32[272,128]{1,0:T(8,128)S(1)}, f32[272,128]{1,0:T(8,128)S(1)}, u32[]{:S(2)}, u32[]{:S(2)}) collective-permute-start(f32[272,128]{1,0:T(8,128)S(1)} %pad_maximum_fusion.3), channel_id=1, source_target_pairs={{24,0},{7,1},{26,2},{1,3},{28,4},{3,5},{30,6},{5,7},{0,8},{15,9},{... | collective-permute-start | bytes 417800 | tf_op jit(solution)/shard_map/ppermute | solution.py:318
  28.0 5.8 %collective-permute-start.7 = (f32[272,128]{1,0:T(8,128)S(1)}, f32[272,128]{1,0:T(8,128)S(1)}, u32[]{:S(2)}, u32[]{:S(2)}) collective-permute-start(f32[272,128]{1,0:T(8,128)S(1)} %pad_maximum_fusion.3), channel_id=1, source_target_pairs={{8,0},{3,1},{10,2},{5,3},{12,4},{7,5},{14,6},{1,7},{16,8},{11,9},{... | collective-permute-start | bytes 417800 | tf_op jit(solution)/shard_map/ppermute | solution.py:318
  30.2 6.6 %collective-permute-start.6 = (f32[272,128]{1,0:T(8,128)S(1)}, f32[272,128]{1,0:T(8,128)S(1)}, u32[]{:S(2)}, u32[]{:S(2)}) collective-permute-start(f32[272,128]{1,0:T(8,128)S(1)} %pad_maximum_fusion.3), channel_id=1, source_target_pairs={{16,0},{5,1},{18,2},{7,3},{20,4},{1,5},{22,6},{3,7},{24,8},{13,9},... | collective-permute-start | bytes 417800 | tf_op jit(solution)/shard_map/ppermute | solution.py:318
  31.7 8.2 %collective-permute-start.9 = (f32[32,2048]{1,0:T(8,128)S(1)}, f32[32,2048]{1,0:T(8,128)S(1)}, u32[]{:S(2)}, u32[]{:S(2)}) collective-permute-start(f32[32,2048]{1,0:T(8,128)S(1)} %pad_maximum_fusion.1), channel_id=1, source_target_pairs={{32,0},{33,1},{34,2},{35,3},{36,4},{37,5},{38,6},{39,7},{40,8},{41... | collective-permute-start | bytes 786440 | tf_op jit(solution)/shard_map/ppermute | solution.py:318
  39.8 9.3 %collective-permute-start.10 = (f32[272,128]{1,0:T(8,128)S(1)}, f32[272,128]{1,0:T(8,128)S(1)}, u32[]{:S(2)}, u32[]{:S(2)}) collective-permute-start(f32[272,128]{1,0:T(8,128)S(1)} %pad_maximum_fusion.4), channel_id=1, source_target_pairs={{128,0},{129,1},{130,2},{131,3},{132,4},{133,5},{134,6},{135,7},{1... | collective-permute-start | bytes 417800 | tf_op jit(solution)/shard_map/ppermute | solution.py:318
  49.1 11.9 %collective-permute-start.13 = (f32[272,128]{1,0:T(8,128)S(1)}, f32[272,128]{1,0:T(8,128)S(1)}, u32[]{:S(2)}, u32[]{:S(2)}) collective-permute-start(f32[272,128]{1,0:T(8,128)S(1)} %pad_maximum_fusion.5), channel_id=1, source_target_pairs={{224,0},{225,1},{226,2},{227,3},{228,4},{229,5},{230,6},{231,7},{2... | collective-permute-start | bytes 417800 | tf_op jit(solution)/shard_map/ppermute | solution.py:318
  53.1 10.8 %collective-permute-start.12 = (f32[272,128]{1,0:T(8,128)S(1)}, f32[272,128]{1,0:T(8,128)S(1)}, u32[]{:S(2)}, u32[]{:S(2)}) collective-permute-start(f32[272,128]{1,0:T(8,128)S(1)} %pad_maximum_fusion.5), channel_id=1, source_target_pairs={{32,0},{33,1},{34,2},{35,3},{36,4},{37,5},{38,6},{39,7},{40,8},{41... | collective-permute-start | bytes 417800 | tf_op jit(solution)/shard_map/ppermute | solution.py:318
  53.1 11.6 %collective-permute-start.11 = (f32[272,128]{1,0:T(8,128)S(1)}, f32[272,128]{1,0:T(8,128)S(1)}, u32[]{:S(2)}, u32[]{:S(2)}) collective-permute-start(f32[272,128]{1,0:T(8,128)S(1)} %pad_maximum_fusion.5), channel_id=1, source_target_pairs={{64,0},{65,1},{66,2},{67,3},{68,4},{69,5},{70,6},{71,7},{72,8},{73... | collective-permute-start | bytes 417800 | tf_op jit(solution)/shard_map/ppermute | solution.py:318
  57.7 49.9 %copy-start = (f32[64,2048]{1,0:T(8,128)}, f32[64,2048]{1,0:T(8,128)S(1)}, u32[]{:S(2)}) copy-start(f32[64,2048]{1,0:T(8,128)S(1)} %pad_maximum_fusion.own_ref) | copy-start | bytes 1572868
  57.7 25.2 %collective-permute-start.15 = (f32[64,2048]{1,0:T(8,128)S(1)}, f32[64,2048]{1,0:T(8,128)S(1)}, u32[]{:S(2)}, u32[]{:S(2)}) collective-permute-start(f32[64,2048]{1,0:T(8,128)S(1)} %pad_maximum_fusion.own_ref), channel_id=1, source_target_pairs={{24,0},{25,1},{26,2},{27,3},{28,4},{29,5},{30,6},{31,7},{0,8},{1,9... | collective-permute-start | bytes 1572872 | tf_op jit(solution)/shard_map/ppermute | solution.py:318
  58.3 24.6 %collective-permute-start.16 = (f32[64,2048]{1,0:T(8,128)S(1)}, f32[64,2048]{1,0:T(8,128)S(1)}, u32[]{:S(2)}, u32[]{:S(2)}) collective-permute-start(f32[64,2048]{1,0:T(8,128)S(1)} %pad_maximum_fusion.own_ref), channel_id=1, source_target_pairs={{8,0},{9,1},{10,2},{11,3},{12,4},{13,5},{14,6},{15,7},{16,8},{17,9... | collective-permute-start | bytes 1572872 | tf_op jit(solution)/shard_map/ppermute | solution.py:318
  61.1 46.6 %collective-permute-start.17 = (f32[64,2048]{1,0:T(8,128)S(1)}, f32[64,2048]{1,0:T(8,128)S(1)}, u32[]{:S(2)}, u32[]{:S(2)}) collective-permute-start(f32[64,2048]{1,0:T(8,128)S(1)} %pad_maximum_fusion.own_ref), channel_id=1, source_target_pairs={{16,0},{17,1},{18,2},{19,3},{20,4},{21,5},{22,6},{23,7},{24,8},{25... | collective-permute-start | bytes 1572872 | tf_op jit(solution)/shard_map/ppermute | solution.py:318
  64.8 18.2 %copy-start.4 = (f32[272,128]{1,0:T(8,128)}, f32[272,128]{1,0:T(8,128)S(1)}, u32[]{:S(2)}) copy-start(f32[272,128]{1,0:T(8,128)S(1)} %pad_maximum_fusion.6.mine_ref) | copy-start | bytes 417796
  64.8 1.4 %collective-permute-start.14 = (f32[272,128]{1,0:T(8,128)S(1)}, f32[272,128]{1,0:T(8,128)S(1)}, u32[]{:S(2)}, u32[]{:S(2)}) collective-permute-start(f32[272,128]{1,0:T(8,128)S(1)} %pad_maximum_fusion.6.mine_ref), channel_id=1, source_target_pairs={{1,0},{0,1},{3,2},{2,3},{5,4},{4,5},{7,6},{6,7},{9,8},{8,9},{11,10... | collective-permute-start | bytes 417800 | tf_op jit(solution)/shard_map/ppermute | solution.py:318
  66.3 16.7 %copy-start.6 = (f32[272,128]{1,0:T(8,128)}, f32[272,128]{1,0:T(8,128)S(1)}, u32[]{:S(2)}) copy-start(f32[272,128]{1,0:T(8,128)S(1)} %collective-permute-done.14.theirs_ref) | copy-start | bytes 417796
  83.0 24.7 %copy-start.1 = (f32[64,2048]{1,0:T(8,128)}, f32[64,2048]{1,0:T(8,128)S(1)}, u32[]{:S(2)}) copy-start(f32[64,2048]{1,0:T(8,128)S(1)} %collective-permute-done.15.right_ref) | copy-start | bytes 1572868
  83.0 24.6 %copy-start.2 = (f32[64,2048]{1,0:T(8,128)}, f32[64,2048]{1,0:T(8,128)S(1)}, u32[]{:S(2)}) copy-start(f32[64,2048]{1,0:T(8,128)S(1)} %collective-permute-done.16.left_ref) | copy-start | bytes 1572868
  (1 other events, 0.8 us)

commit v2 on v1

--- a/solution.py
+++ b/solution.py
@@ -358,10 +358,10 @@
     swap = pairs(lambda z, y, x, core: (z, y, x, 1 - core))
     other = partner(next_core, 4)
     mine, theirs = gram(core_slices)
-    mine = add_pairs(mine, shifted(theirs, swap))
-    mine, other = tie(mine, other)
+    theirs = shifted(theirs, swap)
     rows = merge(next_core, other, 4)
     other = partner(rows, 2)
+    mine = add_pairs(mine, theirs)
     mine = around(mine, lambda d, z, y, x, core: (z, y, x + d, core) if core == 0 else (z, y + d, x, core))
     mine, other = tie(mine, other)
     rows = merge(rows, other, 2)
@@ -369,6 +369,7 @@
     mine = around(mine, lambda d, z, y, x, core: (z, y, x + d, core) if core == 1 else (z, y + d, x, core))
     mine, other = tie(mine, other)
     rows = merge(rows, other, 1)
+    mine, rows = tie(mine, rows)
     right = beside(rows, -1)
     left = beside(rows, 1)
     far = beside(rows, 2)

time: 111 us -> 106 us (0.955)
  the two profiles are of different devices: /device:TPU:32 before, /device:TPU:24 now
where the time goes in v2:
time: 106 us
  waiting for transfers between devices  43.2 us (41%)
  Pallas kernels  32 us (30%)
  starting transfers between devices  28.4 us (27%)
    ppermute x18, waiting for transfers between devices, shifted(): return lax.ppermute(value, ('wide', 'qa', 'qb'), pairs)  43.2 us
    ppermute x18, starting transfers between devices, shifted(): return lax.ppermute(value, ('wide', 'qa', 'qb'), pairs)  28.4 us
    pallas_call x1, Pallas kernels, per_device(): ortho_basis, factor = basis(*total, core_slices)  24.4 us
    pallas_call x1, Pallas kernels, sum_and_spread(): mine, theirs = gram(core_slices)  4.84 us
    pallas_call x1, Pallas kernels, per_device(): pl.pallas_call(next_kernel, out_shape=jax.ShapeDtypeStruct(next_core.shap...  2.66 us
  transfers between devices with their start and end apart: 18, of which 11 were waited for; matrix products, arithmetic and copies ran while one was open for 0% of the time, Pallas kernels for 28%

profile of v2, /device:TPU:24, one launch (start us, length us, event | category | flops | bytes accessed | tf_op | source)
XLA Modules:
  0.0 105.6 jit_solution(5258132146573779759)
XLA Ops:
  0.6 7.3 %collective-permute-start.4 = (f32[8,2048]{1,0:T(8,128)}, f32[8,2048]{1,0:T(8,128)S(1)}, u32[]{:S(2)}, u32[]{:S(2)}) collective-permute-start(f32[8,2048]{1,0:T(8,128)} %param.3), channel_id=1, source_target_pairs={{128,0},{129,1},{130,2},{131,3},{132,4},{133,5},{134,6},{135,7},{1... | collective-permute-start | bytes 196616 | tf_op jit(solution)/shard_map/ppermute | solution.py:318
  7.9 4.8 %shard_map.41 = (f32[272,128]{1,0:T(8,128)}, f32[272,128]{1,0:T(8,128)}) custom-call(f32[1024,256]{1,0:T(8,128)} %core_ref.3), custom_call_target="tpu_custom_call" | custom-call | flops 1342177280 | bytes 2097152 | tf_op jit(solution)/shard_map/pallas_call | solution.py:360
  12.8 1.5 %collective-permute-done = f32[272,128]{1,0:T(8,128)S(1)} collective-permute-done((f32[272,128]{1,0:T(8,128)}, f32[272,128]{1,0:T(8,128)S(1)}, u32[]{:S(2)}, u32[]{:S(2)}) %collective-permute-start) | collective-permute-done | bytes 139296 | tf_op jit(solution)/shard_map/ppermute | solution.py:318
  14.4 1.6 %collective-permute-start.3 = (f32[272,128]{1,0:T(8,128)S(1)}, f32[272,128]{1,0:T(8,128)S(1)}, u32[]{:S(2)}, u32[]{:S(2)}) collective-permute-start(f32[272,128]{1,0:T(8,128)S(1)} %pad_maximum_fusion.2), channel_id=1, source_target_pairs={{6,0},{25,1},{0,2},{27,3},{2,4},{29,5},{4,6},{31,7},{14,8},{1,9},{... | collective-permute-start | bytes 417800 | tf_op jit(solution)/shard_map/ppermute | solution.py:318
  15.9 1.7 %collective-permute-start.2 = (f32[272,128]{1,0:T(8,128)S(1)}, f32[272,128]{1,0:T(8,128)S(1)}, u32[]{:S(2)}, u32[]{:S(2)}) collective-permute-start(f32[272,128]{1,0:T(8,128)S(1)} %pad_maximum_fusion.2), channel_id=1, source_target_pairs={{2,0},{9,1},{4,2},{11,3},{6,4},{13,5},{0,6},{15,7},{10,8},{17,9},{... | collective-permute-start | bytes 417800 | tf_op jit(solution)/shard_map/ppermute | solution.py:318
  17.7 1.8 %collective-permute-start.1 = (f32[272,128]{1,0:T(8,128)S(1)}, f32[272,128]{1,0:T(8,128)S(1)}, u32[]{:S(2)}, u32[]{:S(2)}) collective-permute-start(f32[272,128]{1,0:T(8,128)S(1)} %pad_maximum_fusion.2), channel_id=1, source_target_pairs={{4,0},{17,1},{6,2},{19,3},{0,4},{21,5},{2,6},{23,7},{12,8},{25,9},... | collective-permute-start | bytes 417800 | tf_op jit(solution)/shard_map/ppermute | solution.py:318
  19.5 1.6 %collective-permute-start.5 = (f32[16,2048]{1,0:T(8,128)S(1)}, f32[16,2048]{1,0:T(8,128)S(1)}, u32[]{:S(2)}, u32[]{:S(2)}) collective-permute-start(f32[16,2048]{1,0:T(8,128)S(1)} %pad_maximum_fusion.7), channel_id=1, source_target_pairs={{64,0},{65,1},{66,2},{67,3},{68,4},{69,5},{70,6},{71,7},{72,8},{73... | collective-permute-start | bytes 393224 | tf_op jit(solution)/shard_map/ppermute | solution.py:318
  21.1 3.2 %collective-permute-done.1 = f32[272,128]{1,0:T(8,128)S(1)} collective-permute-done((f32[272,128]{1,0:T(8,128)S(1)}, f32[272,128]{1,0:T(8,128)S(1)}, u32[]{:S(2)}, u32[]{:S(2)}) %collective-permute-start.1) | collective-permute-done | bytes 139296 | tf_op jit(solution)/shard_map/ppermute | solution.py:318
  24.3 2.5 %collective-permute-done.5 = f32[16,2048]{1,0:T(8,128)S(1)} collective-permute-done((f32[16,2048]{1,0:T(8,128)S(1)}, f32[16,2048]{1,0:T(8,128)S(1)}, u32[]{:S(2)}, u32[]{:S(2)}) %collective-permute-start.5) | collective-permute-done | bytes 131104 | tf_op jit(solution)/shard_map/ppermute | solution.py:318
  26.9 1.5 %collective-permute-start.8 = (f32[272,128]{1,0:T(8,128)S(1)}, f32[272,128]{1,0:T(8,128)S(1)}, u32[]{:S(2)}, u32[]{:S(2)}) collective-permute-start(f32[272,128]{1,0:T(8,128)S(1)} %pad_maximum_fusion.3), channel_id=1, source_target_pairs={{24,0},{7,1},{26,2},{1,3},{28,4},{3,5},{30,6},{5,7},{0,8},{15,9},{... | collective-permute-start | bytes 417800 | tf_op jit(solution)/shard_map/ppermute | solution.py:318
  28.9 1.6 %collective-permute-start.6 = (f32[272,128]{1,0:T(8,128)S(1)}, f32[272,128]{1,0:T(8,128)S(1)}, u32[]{:S(2)}, u32[]{:S(2)}) collective-permute-start(f32[272,128]{1,0:T(8,128)S(1)} %pad_maximum_fusion.3), channel_id=1, source_target_pairs={{16,0},{5,1},{18,2},{7,3},{20,4},{1,5},{22,6},{3,7},{24,8},{13,9},... | collective-permute-start | bytes 417800 | tf_op jit(solution)/shard_map/ppermute | solution.py:318
  31.9 4.2 %collective-permute-done.7 = f32[272,128]{1,0:T(8,128)S(1)} collective-permute-done((f32[272,128]{1,0:T(8,128)S(1)}, f32[272,128]{1,0:T(8,128)S(1)}, u32[]{:S(2)}, u32[]{:S(2)}) %collective-permute-start.7) | collective-permute-done | bytes 139296 | tf_op jit(solution)/shard_map/ppermute | solution.py:318
  36.3 1.9 %collective-permute-done.9 = f32[32,2048]{1,0:T(8,128)S(1)} collective-permute-done((f32[32,2048]{1,0:T(8,128)S(1)}, f32[32,2048]{1,0:T(8,128)S(1)}, u32[]{:S(2)}, u32[]{:S(2)}) %collective-permute-start.9) | collective-permute-done | bytes 262176 | tf_op jit(solution)/shard_map/ppermute | solution.py:318
  39.5 8.5 %collective-permute-done.10 = f32[272,128]{1,0:T(8,128)S(1)} collective-permute-done((f32[272,128]{1,0:T(8,128)S(1)}, f32[272,128]{1,0:T(8,128)S(1)}, u32[]{:S(2)}, u32[]{:S(2)}) %collective-permute-start.10) | collective-permute-done | bytes 139296 | tf_op jit(solution)/shard_map/ppermute | solution.py:318
  48.0 1.6 %collective-permute-start.13 = (f32[272,128]{1,0:T(8,128)S(1)}, f32[272,128]{1,0:T(8,128)S(1)}, u32[]{:S(2)}, u32[]{:S(2)}) collective-permute-start(f32[272,128]{1,0:T(8,128)S(1)} %pad_maximum_fusion.5), channel_id=1, source_target_pairs={{224,0},{225,1},{226,2},{227,3},{228,4},{229,5},{230,6},{231,7},{2... | collective-permute-start | bytes 417800 | tf_op jit(solution)/shard_map/ppermute | solution.py:318
  49.5 1.8 %collective-permute-start.12 = (f32[272,128]{1,0:T(8,128)S(1)}, f32[272,128]{1,0:T(8,128)S(1)}, u32[]{:S(2)}, u32[]{:S(2)}) collective-permute-start(f32[272,128]{1,0:T(8,128)S(1)} %pad_maximum_fusion.5), channel_id=1, source_target_pairs={{32,0},{33,1},{34,2},{35,3},{36,4},{37,5},{38,6},{39,7},{40,8},{41... | collective-permute-start | bytes 417800 | tf_op jit(solution)/shard_map/ppermute | solution.py:318
  51.3 3.7 %collective-permute-start.15 = (f32[64,2048]{1,0:T(8,128)S(1)}, f32[64,2048]{1,0:T(8,128)S(1)}, u32[]{:S(2)}, u32[]{:S(2)}) collective-permute-start(f32[64,2048]{1,0:T(8,128)S(1)} %pad_maximum_fusion.own_ref), channel_id=1, source_target_pairs={{24,0},{25,1},{26,2},{27,3},{28,4},{29,5},{30,6},{31,7},{0,8},{1,9... | collective-permute-start | bytes 1572872 | tf_op jit(solution)/shard_map/ppermute | solution.py:318
  55.0 2.4 %collective-permute-start.17 = (f32[64,2048]{1,0:T(8,128)S(1)}, f32[64,2048]{1,0:T(8,128)S(1)}, u32[]{:S(2)}, u32[]{:S(2)}) collective-permute-start(f32[64,2048]{1,0:T(8,128)S(1)} %pad_maximum_fusion.own_ref), channel_id=1, source_target_pairs={{16,0},{17,1},{18,2},{19,3},{20,4},{21,5},{22,6},{23,7},{24,8},{25... | collective-permute-start | bytes 1572872 | tf_op jit(solution)/shard_map/ppermute | solution.py:318
  57.4 1.5 %collective-permute-done.11 = f32[272,128]{1,0:T(8,128)S(1)} collective-permute-done((f32[272,128]{1,0:T(8,128)S(1)}, f32[272,128]{1,0:T(8,128)S(1)}, u32[]{:S(2)}, u32[]{:S(2)}) %collective-permute-start.11) | collective-permute-done | bytes 139296 | tf_op jit(solution)/shard_map/ppermute | solution.py:318
  59.2 1.3 %collective-permute-done.14.theirs_ref = f32[272,128]{1,0:T(8,128)S(1)} collective-permute-done((f32[272,128]{1,0:T(8,128)S(1)}, f32[272,128]{1,0:T(8,128)S(1)}, u32[]{:S(2)}, u32[]{:S(2)}) %collective-permute-start.14) | collective-permute-done | bytes 139296 | tf_op jit(solution)/shard_map/ppermute | solution.py:318
  60.5 13.8 %collective-permute-done.15.right_ref = f32[64,2048]{1,0:T(8,128)S(1)} collective-permute-done((f32[64,2048]{1,0:T(8,128)S(1)}, f32[64,2048]{1,0:T(8,128)S(1)}, u32[]{:S(2)}, u32[]{:S(2)}) %collective-permute-start.15) | collective-permute-done | bytes 524320 | tf_op jit(solution)/shard_map/ppermute | solution.py:318
  74.3 3.4 %collective-permute-done.16.left_ref = f32[64,2048]{1,0:T(8,128)S(1)} collective-permute-done((f32[64,2048]{1,0:T(8,128)S(1)}, f32[64,2048]{1,0:T(8,128)S(1)}, u32[]{:S(2)}, u32[]{:S(2)}) %collective-permute-start.16) | collective-permute-done | bytes 524320 | tf_op jit(solution)/shard_map/ppermute | solution.py:318
  77.7 24.4 %shard_map.42 = (f32[1024,256]{1,0:T(8,128)}, f32[8,256]{1,0:T(8,128)}) custom-call(f32[272,128]{1,0:T(8,128)} %copy-done.5, f32[272,128]{1,0:T(8,128)} %copy-done.7, f32[1024,256]{1,0:T(8,128)} %core_ref.3), custom_call_target="tpu_custom_call" | custom-call | flops 1342177280 | bytes 2097152 | tf_op jit(solution)/shard_map/pallas_call | solution.py:391
  103.0 2.7 %shard_map.43 = f32[8,2048]{1,0:T(8,128)} custom-call(f32[8,256]{1,0:T(8,128)} %get-tuple-element.27.factor_ref, f32[64,2048]{1,0:T(8,128)} %copy-done, f32[64,2048]{1,0:T(8,128)} %copy-done.1, f32[64,2048]{1,0:T(8,128)} %copy-done.2, f32[64,2048]{1,0:T(8,128)} %copy-done.3), custom_call_target="tpu_custom_call" | custom-call | tf_op jit(solution)/shard_map/pallas_call | solution.py:392
  (47 shorter events, 4.4 us)
Async XLA Ops:
  0.6 12.1 %collective-permute-start.4 = (f32[8,2048]{1,0:T(8,128)}, f32[8,2048]{1,0:T(8,128)S(1)}, u32[]{:S(2)}, u32[]{:S(2)}) collective-permute-start(f32[8,2048]{1,0:T(8,128)} %param.3), channel_id=1, source_target_pairs={{128,0},{129,1},{130,2},{131,3},{132,4},{133,5},{134,6},{135,7},{1... | collective-permute-start | bytes 196616 | tf_op jit(solution)/shard_map/ppermute | solution.py:318
  7.9 4.9 %copy-start.6 = (f32[8,2048]{1,0:T(8,128)S(1)}, f32[8,2048]{1,0:T(8,128)}, u32[]{:S(2)}) copy-start(f32[8,2048]{1,0:T(8,128)} %param.3) | copy-start | bytes 196612
  12.8 1.6 %collective-permute-start = (f32[272,128]{1,0:T(8,128)}, f32[272,128]{1,0:T(8,128)S(1)}, u32[]{:S(2)}, u32[]{:S(2)}) collective-permute-start(f32[272,128]{1,0:T(8,128)} %get-tuple-element.17), channel_id=1, source_target_pairs={{1,0},{0,1},{3,2},{2,3},{5,4},{4,5},{7,6},{6,7},{9,8},{8,9},{11,10... | collective-permute-start | bytes 417800 | tf_op jit(solution)/shard_map/ppermute | solution.py:318
  14.4 6.7 %collective-permute-start.3 = (f32[272,128]{1,0:T(8,128)S(1)}, f32[272,128]{1,0:T(8,128)S(1)}, u32[]{:S(2)}, u32[]{:S(2)}) collective-permute-start(f32[272,128]{1,0:T(8,128)S(1)} %pad_maximum_fusion.2), channel_id=1, source_target_pairs={{6,0},{25,1},{0,2},{27,3},{2,4},{29,5},{4,6},{31,7},{14,8},{1,9},{... | collective-permute-start | bytes 417800 | tf_op jit(solution)/shard_map/ppermute | solution.py:318
  15.9 5.1 %collective-permute-start.2 = (f32[272,128]{1,0:T(8,128)S(1)}, f32[272,128]{1,0:T(8,128)S(1)}, u32[]{:S(2)}, u32[]{:S(2)}) collective-permute-start(f32[272,128]{1,0:T(8,128)S(1)} %pad_maximum_fusion.2), channel_id=1, source_target_pairs={{2,0},{9,1},{4,2},{11,3},{6,4},{13,5},{0,6},{15,7},{10,8},{17,9},{... | collective-permute-start | bytes 417800 | tf_op jit(solution)/shard_map/ppermute | solution.py:318
  17.7 6.6 %collective-permute-start.1 = (f32[272,128]{1,0:T(8,128)S(1)}, f32[272,128]{1,0:T(8,128)S(1)}, u32[]{:S(2)}, u32[]{:S(2)}) collective-permute-start(f32[272,128]{1,0:T(8,128)S(1)} %pad_maximum_fusion.2), channel_id=1, source_target_pairs={{4,0},{17,1},{6,2},{19,3},{0,4},{21,5},{2,6},{23,7},{12,8},{25,9},... | collective-permute-start | bytes 417800 | tf_op jit(solution)/shard_map/ppermute | solution.py:318
  19.5 7.4 %collective-permute-start.5 = (f32[16,2048]{1,0:T(8,128)S(1)}, f32[16,2048]{1,0:T(8,128)S(1)}, u32[]{:S(2)}, u32[]{:S(2)}) collective-permute-start(f32[16,2048]{1,0:T(8,128)S(1)} %pad_maximum_fusion.7), channel_id=1, source_target_pairs={{64,0},{65,1},{66,2},{67,3},{68,4},{69,5},{70,6},{71,7},{72,8},{73... | collective-permute-start | bytes 393224 | tf_op jit(solution)/shard_map/ppermute | solution.py:318
  26.9 5.1 %collective-permute-start.8 = (f32[272,128]{1,0:T(8,128)S(1)}, f32[272,128]{1,0:T(8,128)S(1)}, u32[]{:S(2)}, u32[]{:S(2)}) collective-permute-start(f32[272,128]{1,0:T(8,128)S(1)} %pad_maximum_fusion.3), channel_id=1, source_target_pairs={{24,0},{7,1},{26,2},{1,3},{28,4},{3,5},{30,6},{5,7},{0,8},{15,9},{... | collective-permute-start | bytes 417800 | tf_op jit(solution)/shard_map/ppermute | solution.py:318
  28.4 7.8 %collective-permute-start.7 = (f32[272,128]{1,0:T(8,128)S(1)}, f32[272,128]{1,0:T(8,128)S(1)}, u32[]{:S(2)}, u32[]{:S(2)}) collective-permute-start(f32[272,128]{1,0:T(8,128)S(1)} %pad_maximum_fusion.3), channel_id=1, source_target_pairs={{8,0},{3,1},{10,2},{5,3},{12,4},{7,5},{14,6},{1,7},{16,8},{11,9},{... | collective-permute-start | bytes 417800 | tf_op jit(solution)/shard_map/ppermute | solution.py:318
  28.9 7.3 %collective-permute-start.6 = (f32[272,128]{1,0:T(8,128)S(1)}, f32[272,128]{1,0:T(8,128)S(1)}, u32[]{:S(2)}, u32[]{:S(2)}) collective-permute-start(f32[272,128]{1,0:T(8,128)S(1)} %pad_maximum_fusion.3), channel_id=1, source_target_pairs={{16,0},{5,1},{18,2},{7,3},{20,4},{1,5},{22,6},{3,7},{24,8},{13,9},... | collective-permute-start | bytes 417800 | tf_op jit(solution)/shard_map/ppermute | solution.py:318
  30.6 7.6 %collective-permute-start.9 = (f32[32,2048]{1,0:T(8,128)S(1)}, f32[32,2048]{1,0:T(8,128)S(1)}, u32[]{:S(2)}, u32[]{:S(2)}) collective-permute-start(f32[32,2048]{1,0:T(8,128)S(1)} %pad_maximum_fusion.1), channel_id=1, source_target_pairs={{32,0},{33,1},{34,2},{35,3},{36,4},{37,5},{38,6},{39,7},{40,8},{41... | collective-permute-start | bytes 786440 | tf_op jit(solution)/shard_map/ppermute | solution.py:318
  38.3 20.8 %copy-start = (f32[64,2048]{1,0:T(8,128)}, f32[64,2048]{1,0:T(8,128)S(1)}, u32[]{:S(2)}) copy-start(f32[64,2048]{1,0:T(8,128)S(1)} %pad_maximum_fusion.own_ref) | copy-start | bytes 1572868
  38.3 9.7 %collective-permute-start.10 = (f32[272,128]{1,0:T(8,128)S(1)}, f32[272,128]{1,0:T(8,128)S(1)}, u32[]{:S(2)}, u32[]{:S(2)}) collective-permute-start(f32[272,128]{1,0:T(8,128)S(1)} %pad_maximum_fusion.4), channel_id=1, source_target_pairs={{128,0},{129,1},{130,2},{131,3},{132,4},{133,5},{134,6},{135,7},{1... | collective-permute-start | bytes 417800 | tf_op jit(solution)/shard_map/ppermute | solution.py:318
  48.0 7.0 %collective-permute-start.13 = (f32[272,128]{1,0:T(8,128)S(1)}, f32[272,128]{1,0:T(8,128)S(1)}, u32[]{:S(2)}, u32[]{:S(2)}) collective-permute-start(f32[272,128]{1,0:T(8,128)S(1)} %pad_maximum_fusion.5), channel_id=1, source_target_pairs={{224,0},{225,1},{226,2},{227,3},{228,4},{229,5},{230,6},{231,7},{2... | collective-permute-start | bytes 417800 | tf_op jit(solution)/shard_map/ppermute | solution.py:318
  49.5 7.9 %collective-permute-start.12 = (f32[272,128]{1,0:T(8,128)S(1)}, f32[272,128]{1,0:T(8,128)S(1)}, u32[]{:S(2)}, u32[]{:S(2)}) collective-permute-start(f32[272,128]{1,0:T(8,128)S(1)} %pad_maximum_fusion.5), channel_id=1, source_target_pairs={{32,0},{33,1},{34,2},{35,3},{36,4},{37,5},{38,6},{39,7},{40,8},{41... | collective-permute-start | bytes 417800 | tf_op jit(solution)/shard_map/ppermute | solution.py:318
  51.3 7.6 %collective-permute-start.11 = (f32[272,128]{1,0:T(8,128)S(1)}, f32[272,128]{1,0:T(8,128)S(1)}, u32[]{:S(2)}, u32[]{:S(2)}) collective-permute-start(f32[272,128]{1,0:T(8,128)S(1)} %pad_maximum_fusion.5), channel_id=1, source_target_pairs={{64,0},{65,1},{66,2},{67,3},{68,4},{69,5},{70,6},{71,7},{72,8},{73... | collective-permute-start | bytes 417800 | tf_op jit(solution)/shard_map/ppermute | solution.py:318
  51.3 23.0 %collective-permute-start.15 = (f32[64,2048]{1,0:T(8,128)S(1)}, f32[64,2048]{1,0:T(8,128)S(1)}, u32[]{:S(2)}, u32[]{:S(2)}) collective-permute-start(f32[64,2048]{1,0:T(8,128)S(1)} %pad_maximum_fusion.own_ref), channel_id=1, source_target_pairs={{24,0},{25,1},{26,2},{27,3},{28,4},{29,5},{30,6},{31,7},{0,8},{1,9... | collective-permute-start | bytes 1572872 | tf_op jit(solution)/shard_map/ppermute | solution.py:318
  55.0 22.7 %collective-permute-start.16 = (f32[64,2048]{1,0:T(8,128)S(1)}, f32[64,2048]{1,0:T(8,128)S(1)}, u32[]{:S(2)}, u32[]{:S(2)}) collective-permute-start(f32[64,2048]{1,0:T(8,128)S(1)} %pad_maximum_fusion.own_ref), channel_id=1, source_target_pairs={{8,0},{9,1},{10,2},{11,3},{12,4},{13,5},{14,6},{15,7},{16,8},{17,9... | collective-permute-start | bytes 1572872 | tf_op jit(solution)/shard_map/ppermute | solution.py:318
  55.0 47.2 %collective-permute-start.17 = (f32[64,2048]{1,0:T(8,128)S(1)}, f32[64,2048]{1,0:T(8,128)S(1)}, u32[]{:S(2)}, u32[]{:S(2)}) collective-permute-start(f32[64,2048]{1,0:T(8,128)S(1)} %pad_maximum_fusion.own_ref), channel_id=1, source_target_pairs={{16,0},{17,1},{18,2},{19,3},{20,4},{21,5},{22,6},{23,7},{24,8},{25... | collective-permute-start | bytes 1572872 | tf_op jit(solution)/shard_map/ppermute | solution.py:318
  59.0 18.7 %copy-start.5 = (f32[272,128]{1,0:T(8,128)}, f32[272,128]{1,0:T(8,128)S(1)}, u32[]{:S(2)}) copy-start(f32[272,128]{1,0:T(8,128)S(1)} %pad_maximum_fusion.6.mine_ref) | copy-start | bytes 417796
  59.1 1.4 %collective-permute-start.14 = (f32[272,128]{1,0:T(8,128)S(1)}, f32[272,128]{1,0:T(8,128)S(1)}, u32[]{:S(2)}, u32[]{:S(2)}) collective-permute-start(f32[272,128]{1,0:T(8,128)S(1)} %pad_maximum_fusion.6.mine_ref), channel_id=1, source_target_pairs={{1,0},{0,1},{3,2},{2,3},{5,4},{4,5},{7,6},{6,7},{9,8},{8,9},{11,10... | collective-permute-start | bytes 417800 | tf_op jit(solution)/shard_map/ppermute | solution.py:318
  60.5 17.2 %copy-start.7 = (f32[272,128]{1,0:T(8,128)}, f32[272,128]{1,0:T(8,128)S(1)}, u32[]{:S(2)}) copy-start(f32[272,128]{1,0:T(8,128)S(1)} %collective-permute-done.14.theirs_ref) | copy-start | bytes 417796
  74.3 27.8 %copy-start.1 = (f32[64,2048]{1,0:T(8,128)}, f32[64,2048]{1,0:T(8,128)S(1)}, u32[]{:S(2)}) copy-start(f32[64,2048]{1,0:T(8,128)S(1)} %collective-permute-done.15.right_ref) | copy-start | bytes 1572868
  77.7 24.5 %copy-start.2 = (f32[64,2048]{1,0:T(8,128)}, f32[64,2048]{1,0:T(8,128)S(1)}, u32[]{:S(2)}) copy-start(f32[64,2048]{1,0:T(8,128)S(1)} %collective-permute-done.16.left_ref) | copy-start | bytes 1572868
  (2 other events, 2.4 us)
